TPU v7x, 512 devices: a whole 4x4x16 slice. The times are simulated.
512 devices in a mesh: dp: 4 (over y), pipe: 16 (over z_hi, x, core), tensor: 8 (over z_lo).
Axes of the slice: x: 4, y: 4, z: 16 (z_hi: 2, z_lo: 8; z = z_hi * 8 + z_lo), core: 2. Of those that a mesh axis runs over, the one named last changes fastest.
Arguments:
- enc_out: bfloat16 [512, 4096], P('dp', 'tensor'), may hold values from -1.25 to 1.25
- mlp_input: bfloat16 [512, 4096], P('dp', 'tensor'), may hold values from -170 to 170
- grad_kv: bfloat16 [512, 2, 16, 2048], P('dp', None, 'pipe', 'tensor'), may hold values from -1.5 to 1.5
- kv_weight: bfloat16 [4096, 2, 16, 2048], P('dp', None, 'pipe', 'tensor'), may hold values from -0.09375 to 0.09375
- gate_weight: bfloat16 [4096, 16384], P('dp', ('pipe', 'tensor')), may hold values from -0.09375 to 0.09375
- up_weight: bfloat16 [4096, 16384], P('dp', ('pipe', 'tensor')), may hold values from -0.09375 to 0.09375
- down_weight: bfloat16 [16384, 4096], P(('pipe', 'tensor'), 'dp'), may hold values from -0.046875 to 0.046875
- norm_gain: bfloat16 [4096], replicated, may hold values from 0.099609375 to 1.8984375
Outputs:
- input_grad: bfloat16 [512, 4096], P('dp')
- kv_grad: bfloat16 [4096, 2, 16, 2048], P('dp', None, 'pipe', 'tensor')
All inputs are finite; a program needn't handle non-finite values.
Results may differ from a plain program's by a relative error of at most 0.009.
Values may be sent and summed in bfloat16 or wider, within the bound.
A program may use at most 64 MiB of HBM per device.

v0:
```python
import math

import jax
import jax.numpy as jnp
from jax import lax
from jax.sharding import PartitionSpec as P


def gelu_parts(preact):
    factor = math.sqrt(2.0 / math.pi)
    tangent = jnp.tanh(factor * (preact + 0.044715 * preact * preact * preact))
    gelu_value = 0.5 * preact * (1.0 + tangent)
    gelu_slope = 0.5 * (1.0 + tangent) + 0.5 * preact * (1.0 - tangent * tangent) * factor * (
        1.0 + 3.0 * 0.044715 * preact * preact
    )
    return (gelu_value, gelu_slope)


def on_device(
    enc_out, mlp_input, grad_kv, kv_weight, gate_weight, up_weight, down_weight, norm_gain
):
    encoded, resid_full = (
        lax.all_gather(enc_out, "tensor", axis=1, tiled=True),
        lax.all_gather(mlp_input, "tensor", axis=1, tiled=True),
    )
    partial_value = jnp.einsum(
        "tslc,dslc->td",
        grad_kv,
        lax.all_gather(kv_weight, "dp", axis=0, tiled=True),
        preferred_element_type=jnp.float32,
    )
    gate_full, up_full, down_full = (
        lax.all_gather(gate_weight, "dp", axis=0, tiled=True),
        lax.all_gather(up_weight, "dp", axis=0, tiled=True),
        lax.all_gather(down_weight, "dp", axis=1, tiled=True),
    )
    values_in = resid_full.astype(jnp.float32)
    row_scale = lax.rsqrt(jnp.mean(values_in * values_in, axis=1, keepdims=True) + 1e-06)
    gain_row = norm_gain.astype(jnp.float32)
    normed = (values_in * row_scale * gain_row).astype(jnp.bfloat16)
    gate_pre = jnp.dot(normed, gate_full, preferred_element_type=jnp.float32)
    up_pre = jnp.dot(normed, up_full, preferred_element_type=jnp.float32)
    upstream = lax.psum(partial_value, ("pipe", "tensor"))
    upstream_half = upstream.astype(jnp.bfloat16)
    contract = (((1,), (1,)), ((), ()))
    hidden_grad = lax.dot_general(
        upstream_half, down_full, contract, preferred_element_type=jnp.float32
    )
    gelu_value, gelu_slope = gelu_parts(gate_pre)
    gate_grad = (hidden_grad * up_pre * gelu_slope).astype(jnp.bfloat16)
    up_grad = (hidden_grad * gelu_value).astype(jnp.bfloat16)
    normed_part = lax.dot_general(
        gate_grad, gate_full, contract, preferred_element_type=jnp.float32
    ) + lax.dot_general(up_grad, up_full, contract, preferred_element_type=jnp.float32)
    normed_grad = lax.psum(normed_part, ("pipe", "tensor"))
    scaled_grad = gain_row * normed_grad
    input_full = (
        upstream
        + row_scale * scaled_grad
        - values_in
        * (row_scale * row_scale * row_scale)
        * jnp.mean(values_in * scaled_grad, axis=1, keepdims=True)
    )
    input_grad = input_full.astype(jnp.bfloat16)
    kv_grad = lax.psum_scatter(
        jnp.einsum("td,tslc->dslc", encoded, grad_kv, preferred_element_type=jnp.float32).astype(
            jnp.bfloat16
        ),
        "dp",
        scatter_dimension=0,
        tiled=True,
    )
    return (input_grad, kv_grad)


def solution(mesh):
    placed = (
        P("dp", "tensor"),
        P("dp", "tensor"),
        P("dp", None, "pipe", "tensor"),
        P("dp", None, "pipe", "tensor"),
        P("dp", ("pipe", "tensor")),
        P("dp", ("pipe", "tensor")),
        P(("pipe", "tensor"), "dp"),
        P(),
    )
    return jax.shard_map(
        on_device,
        mesh=mesh,
        in_specs=placed,
        out_specs=(P("dp", None), P("dp", None, "pipe", "tensor")),
        check_vma=False,
    )
```

profile of v0, /device:TPU:1, one launch (start us, length us, event | category | flops | bytes accessed | tf_op | source)
XLA Modules:
  0.0 1073.9 jit_solution(2873220587670729646)
XLA Ops:
  7.2 2.4 copy.10
  9.6 0.0 all-gather.9.cloned.1.call-start
  9.7 0.7 all-gather.9.cloned.1.call-update
  10.4 0.7 all-gather.15.cloned.1.call-update
  11.1 0.5 all-gather.11.cloned.1.call-update
  11.7 0.0 all-reduce.3.cloned.1.call-start
  11.7 60.0 %all-gather.7.cloned.1.call-done = bf16[4096,2,1,256]{3,0,1,2:T(8,128)(2,1)} async-done(((bf16[1024,2,1,256]{3,0,1,2:T(8,128)(2,1)}), bf16[4096,2,1,256]{3,0,1,2:T(8,128)(2,1)}) %all-gather.7.cloned.1.call-update) | async-done | bytes 4194320 | tf_op jit(solution)/shard_map/all_gather | solution.py:29
  71.7 5.0 convolution_bitcast_fusion
  76.8 0.0 all-gather.13.cloned.1.call-start
  76.8 0.5 all-gather.13.cloned.1.call-update
  77.3 0.0 all-gather.17.cloned.1.call-start
  77.4 0.2 copy-done.3
  77.6 0.8 copy.12
  78.4 0.0 all-reduce.5.cloned.1.call-start
  78.5 56.7 %all-gather.9.cloned.1.call-done = bf16[128,4096]{1,0:T(8,128)(2,1)} async-done(((bf16[128,512]{1,0:T(8,128)(2,1)}), bf16[128,4096]{1,0:T(8,128)(2,1)}) %all-gather.9.cloned.1.call-update) | async-done | bytes 1048592 | tf_op jit(solution)/shard_map/all_gather | solution.py:24
  135.2 1.5 fusion.2
  136.7 30.8 %all-gather.15.cloned.1.call-done = bf16[4096,128]{1,0:T(8,128)(2,1)} async-done(((bf16[1024,128]{1,0:T(8,128)(2,1)}), bf16[4096,128]{1,0:T(8,128)(2,1)}) %all-gather.15.cloned.1.call-update) | async-done | bytes 1048592 | tf_op jit(solution)/shard_map/all_gather | solution.py:33
  167.5 2.0 fusion.15
  169.6 32.1 %all-gather.11.cloned.1.call-done = bf16[128,4096]{1,0:T(8,128)(2,1)} async-done(((bf16[128,1024]{1,0:T(8,128)(2,1)}), bf16[128,4096]{1,0:T(8,128)(2,1)}) %all-gather.11.cloned.1.call-update) | async-done | bytes 1048592 | tf_op jit(solution)/shard_map/all_gather | solution.py:35
  201.7 355.8 %all-reduce.3.cloned.1.call-done = f32[128,4096]{1,0:T(8,128)} async-done(((f32[128,4096]{1,0:T(8,128)}), f32[128,4096]{1,0:T(8,128)}) %all-reduce.3.cloned.1.call-update) | async-done | bytes 2097168 | tf_op jit(solution)/shard_map/psum | solution.py:43
  557.5 2.3 fusion.13
  559.8 28.0 %all-gather.13.cloned.1.call-done = bf16[4096,128]{1,0:T(8,128)(2,1)} async-done(((bf16[1024,128]{1,0:T(8,128)(2,1)}), bf16[4096,128]{1,0:T(8,128)(2,1)}) %all-gather.13.cloned.1.call-update) | async-done | bytes 1048592 | tf_op jit(solution)/shard_map/all_gather | solution.py:34
  587.8 2.4 fusion.11
  590.2 3.1 convolution_add_fusion
  593.3 0.0 reduce-scatter.2.cloned.1.call-start
  593.4 60.3 %all-gather.17.cloned.1.call-done = bf16[128,4096]{0,1:T(8,128)(2,1)} async-done(((bf16[128,512]{0,1:T(8,128)(2,1)}), bf16[128,4096]{0,1:T(8,128)(2,1)}) %all-gather.17.cloned.1.call-update) | async-done | bytes 1048592 | tf_op jit(solution)/shard_map/all_gather | solution.py:23
  653.7 4.4 fusion
  658.1 350.1 %all-reduce.5.cloned.1.call-done = f32[128,4096]{1,0:T(8,128)} async-done(((f32[128,4096]{1,0:T(8,128)}), f32[128,4096]{1,0:T(8,128)}) %all-reduce.5.cloned.1.call-update) | async-done | bytes 2097168 | tf_op jit(solution)/shard_map/psum | solution.py:55
  1008.2 1.9 fusion.8
  1010.1 3.3 fusion.7
  1013.5 50.7 %reduce-scatter.2.cloned.1.call-done = bf16[1024,2,1,256]{3,0,1,2:T(8,128)(2,1)} async-done(((bf16[4096,2,1,256]{3,0,1,2:T(8,128)(2,1)}), bf16[1024,2,1,256]{3,0,1,2:T(8,128)(2,1)}) %reduce-scatter.2.cloned.1.call-update) | async-done | bytes 1048592 | tf_op jit(solution)/shard_map/reduce_scatter | solution.py:65
  1064.1 3.3 copy.14
  (20 shorter events, 0.2 us)
Async XLA Ops:
  7.2 64.6 %copy-start.2 = (bf16[128,2,1,256]{3,1,2,0:T(2,128)(2,1)S(1)}, bf16[128,2,1,256]{3,1,2,0:T(2,128)(2,1)}, u32[]{:S(2)}) copy-start(bf16[128,2,1,256]{3,1,2,0:T(2,128)(2,1)} %param.10) | copy-start | bytes 393220
  7.2 64.5 %all-gather.7.cloned.1.call-start = ((), (), s32[]{:S(2)}) async-start(), calls=%async_computation.1 | async-start | bytes 5242880 | tf_op jit(solution)/shard_map/all_gather | solution.py:29
  9.6 125.6 %all-gather.9.cloned.1.call-start = ((), (), s32[]{:S(2)}) async-start(), calls=%async_computation.3 | async-start | bytes 1179648 | tf_op jit(solution)/shard_map/all_gather | solution.py:24
  10.4 157.2 %all-gather.15.cloned.1.call-start = ((), (), s32[]{:S(2)}) async-start(), calls=%async_computation.6 | async-start | bytes 1310720 | tf_op jit(solution)/shard_map/all_gather | solution.py:33
  11.1 190.6 %all-gather.11.cloned.1.call-start = ((), (), s32[]{:S(2)}) async-start(), calls=%async_computation.4 | async-start | bytes 1310720 | tf_op jit(solution)/shard_map/all_gather | solution.py:35
  11.7 545.8 %all-reduce.3.cloned.1.call-start = ((), (), s32[]{:S(2)}) async-start(), calls=%async_computation.2 | async-start | bytes 4194304 | tf_op jit(solution)/shard_map/psum | solution.py:43
  76.7 0.9 copy-start.3
  76.7 1.7 copy-start.4
  76.8 511.0 %all-gather.13.cloned.1.call-start = ((), (), s32[]{:S(2)}) async-start(), calls=%async_computation.5 | async-start | bytes 1310720 | tf_op jit(solution)/shard_map/all_gather | solution.py:34
  77.3 576.3 %all-gather.17.cloned.1.call-start = ((), (), s32[]{:S(2)}) async-start(), calls=%async_computation.8 | async-start | bytes 1179648 | tf_op jit(solution)/shard_map/all_gather | solution.py:23
  78.4 929.7 %all-reduce.5.cloned.1.call-start = ((), (), s32[]{:S(2)}) async-start(), calls=%async_computation.7 | async-start | bytes 4194304 | tf_op jit(solution)/shard_map/psum | solution.py:55
  169.6 418.2 %copy-start = (bf16[128,4096]{1,0:T(8,128)(2,1)S(1)}, bf16[128,4096]{1,0:T(8,128)(2,1)}, u32[]{:S(2)}) copy-start(bf16[128,4096]{1,0:T(8,128)(2,1)} %all-gather.9.cloned.1.call-done) | copy-start | bytes 3145732
  593.3 470.8 %reduce-scatter.2.cloned.1.call-start = ((), (), s32[]{:S(2)}) async-start(), calls=%async_computation.9 | async-start | bytes 5242880 | tf_op jit(solution)/shard_map/reduce_scatter | solution.py:65
  658.1 352.0 %copy-start.1 = (f32[128,4096]{1,0:T(8,128)S(1)}, f32[128,4096]{1,0:T(8,128)}, u32[]{:S(2)}) copy-start(f32[128,4096]{1,0:T(8,128)} %all-reduce.3.cloned.1.call-done) | copy-start | bytes 6291460
Sparse Core Ops, SparseCore 0:
  10.7 61.0 all-gather.6
  73.8 61.3 all-gather.8
  137.3 30.1 all-gather.14
  169.5 32.1 all-gather.10
  205.0 352.4 all-reduce.2
  559.5 28.3 all-gather.12
  590.5 63.1 all-gather.16
  657.1 351.0 all-reduce.4
  1011.0 53.0 reduce-scatter.1
where the time goes:
time: 1070 us
  waiting for transfers between devices  1030 us (96%)
  matrix products  19.3 us (2%)
  between operations  13.9 us (1%)
    psum x1, waiting for transfers between devices, on_device(): upstream = lax.psum(partial_value, ('pipe', 'tensor'))  356 us
    psum x1, waiting for transfers between devices, on_device(): normed_grad = lax.psum(normed_part, ('pipe', 'tensor'))  350 us
    all_gather x1, waiting for transfers between devices, on_device(): lax.all_gather(enc_out, 'tensor', axis=1, tiled=True)  60.3 us
    all_gather x1, waiting for transfers between devices, on_device(): lax.all_gather(kv_weight, 'dp', axis=0, tiled=True)  60 us
    all_gather x1, waiting for transfers between devices, on_device(): lax.all_gather(mlp_input, 'tensor', axis=1, tiled=True)  56.7 us
    reduce_scatter x1, waiting for transfers between devices, on_device(): lax.psum_scatter(jnp.einsum('td,tslc->dslc', encoded, grad_kv, preferred_...  50.7 us
    all_gather x1, waiting for transfers between devices, on_device(): lax.all_gather(down_weight, 'dp', axis=1, tiled=True)  32.1 us
    all_gather x1, waiting for transfers between devices, on_device(): lax.all_gather(gate_weight, 'dp', axis=0, tiled=True)  30.8 us
  transfers between devices with their start and end apart: 9, of which 9 were waited for; matrix products, arithmetic and copies ran while one was open for 2% of the time, Pallas kernels for 0%

commit v1 on v0

v1 whole, which is shorter than its diff:
```python
import math

import jax
import jax.numpy as jnp
from jax import lax
from jax.experimental import pallas as pl
from jax.experimental.pallas import tpu as pltpu
from jax.sharding import PartitionSpec as P

MESH = pl.DeviceIdType.MESH
F32, BF16 = jnp.float32, jnp.bfloat16
NT = (((1,), (1,)), ((), ()))
TN = (((0,), (0,)), ((), ()))


def gelu_parts(preact):
    factor = math.sqrt(2.0 / math.pi)
    tangent = jnp.tanh(factor * (preact + 0.044715 * preact * preact * preact))
    gelu_value = 0.5 * preact * (1.0 + tangent)
    gelu_slope = 0.5 * (1.0 + tangent) + 0.5 * preact * (1.0 - tangent * tangent) * factor * (
        1.0 + 3.0 * 0.044715 * preact * preact
    )
    return (gelu_value, gelu_slope)


def at(index, size):
    return pl.ds(pl.multiple_of(index * size, size), size)


def kernel(
    enc, mlp, grad, kvw, gate, up, down, gain, out, kvg,
    gall, kvv, usend, uown, crecv, xsend, xrecv, ysend, yb, zrecv, upf, ub,
    gu, db, xb, nb, rsb, eb, ee, act, pre, gg, psend, pown, pcrecv, pxsend, pxrecv, pzsend, pzrecv,
    lsem, gsem, wsem, msem, esem, mxsem, mcsem, rcsem, rxsem, rysem, rzsem, azsem, axsem, acsem,
):
    y, pipe, t = lax.axis_index("dp"), lax.axis_index("pipe"), lax.axis_index("tensor")
    zh, x, c = lax.div(pipe, 8), lax.rem(lax.div(pipe, 2), 4), lax.rem(pipe, 2)
    z = zh * 8 + t
    rows = pl.ds(pl.multiple_of(c * 64 + x * 16, 16), 16)
    xrows = pl.ds(pl.multiple_of(x * 16, 16), 16)

    def y_at(d):
        return lax.rem(y + d, 4)

    def x_at(d):
        return lax.rem(x + d, 4)

    def z_at(d):
        return lax.rem(z + d, 16)

    def y_dev(d):
        return {"dp": y_at(d)}

    def x_dev(d):
        return {"pipe": zh * 8 + x_at(d) * 2 + c}

    def z_dev(d):
        peer = z_at(d)
        return {"pipe": lax.div(peer, 8) * 8 + x * 2 + c, "tensor": lax.rem(peer, 8)}

    core_dev = {"pipe": pipe + 1 - 2 * c}

    def remote(src, dst, sems, index, device):
        return pltpu.make_async_remote_copy(
            src_ref=src,
            dst_ref=dst,
            send_sem=sems.at[(0,) + index],
            recv_sem=sems.at[(1,) + index],
            device_id=device,
            device_id_type=MESH,
        )

    barrier = pltpu.get_barrier_semaphore()

    def greet(device):
        pl.semaphore_signal(barrier, inc=1, device_id=device, device_id_type=MESH)

    @pl.loop(1, 16)
    def _(d):
        greet(z_dev(d))

    @pl.loop(1, 4)
    def _(d):
        greet(y_dev(d))
        greet(x_dev(d))

    greet(core_dev)

    own = [
        pltpu.make_async_copy(grad.at[at(0, 64)], gall.at[0, y], lsem.at[0]),
        pltpu.make_async_copy(grad.at[at(1, 64)], gall.at[1, y], lsem.at[1]),
        pltpu.make_async_copy(kvw, kvv, lsem.at[2]),
        pltpu.make_async_copy(mlp.at[rows], xb.at[rows, at(t, 512)], lsem.at[3]),
        pltpu.make_async_copy(enc.at[rows], eb.at[:, at(t, 512)], lsem.at[4]),
        pltpu.make_async_copy(gate, gu.at[at(y, 1024), pl.ds(0, 128)], lsem.at[5]),
        pltpu.make_async_copy(up, gu.at[at(y, 1024), pl.ds(128, 128)], lsem.at[6]),
        pltpu.make_async_copy(down, db.at[:, at(y, 1024)], lsem.at[7]),
    ]
    for copy in own:
        copy.start()

    pl.semaphore_wait(barrier, 22)

    def grad_copy(d, h, to):
        return remote(grad.at[at(h, 64)], gall.at[h, to], gsem, (d, h), y_dev(d))

    def weight_copy(k, d, block):
        src, dst = (
            (gate, gu.at[at(block, 1024), pl.ds(0, 128)]),
            (up, gu.at[at(block, 1024), pl.ds(128, 128)]),
            (down, db.at[:, at(block, 1024)]),
        )[k]
        return remote(src, dst, wsem, (k, d), y_dev(d))

    def lo_copy(k, d, block):
        src = (mlp, enc)[k].at[rows]
        dst = (xb.at[rows, at(block, 512)], eb.at[:, at(block, 512)])[k]
        return remote(src, dst, msem, (k, d), {"tensor": lax.rem(t + d, 8)})

    def enc_y_copy(d, frm):
        return remote(eb.at[:, at(y_at(d), 1024)], ee.at[frm, rows, :], esem, (d,), y_dev(d))

    def side_x_copy(k, d, block):
        r = pl.ds(pl.multiple_of(c * 64 + block * 16, 16), 16)
        src = (xb.at[rows, :], ee.at[:, rows, :])[k]
        dst = (xb.at[r, :], ee.at[:, r, :])[k]
        return remote(src, dst, mxsem, (k, d), x_dev(d))

    def side_core_copy(k, half):
        ref = (xb.at[at(c, 64), :], ee.at[:, at(c, 64), :])[k]
        dst = (xb.at[at(half, 64), :], ee.at[:, at(half, 64), :])[k]
        return remote(ref, dst, mcsem, (k,), core_dev)

    def gather_z_copy(k, d, block):
        ref = (ub, out)[k]
        return remote(ref.at[rows, at(z, 256)], ref.at[rows, at(block, 256)], azsem, (k, d), z_dev(d))

    def gather_x_copy(k, d, block):
        ref = (ub, out)[k]
        r = pl.ds(pl.multiple_of(c * 64 + block * 16, 16), 16)
        return remote(ref.at[rows, :], ref.at[r, :], axsem, (k, d), x_dev(d))

    def gather_core_copy(k, d, half):
        ref = (ub, out)[k]
        block = lax.rem(x + 4 - d, 4)
        src = pl.ds(pl.multiple_of(c * 64 + block * 16, 16), 16)
        dst = pl.ds(pl.multiple_of(half * 64 + block * 16, 16), 16)
        return remote(ref.at[src, :], ref.at[dst, :], acsem, (k, d), core_dev)

    def farthest_first(k):
        j = lax.div(k + 1, 2)
        return 8 + j * (1 - 2 * lax.rem(k, 2))

    def gather(k, before_rows=None):
        @pl.loop(0, 15)
        def _(i):
            d = farthest_first(i)
            gather_z_copy(k, d, z).start()

        if before_rows is not None:
            before_rows()

        @pl.loop(1, 16)
        def _(d):
            gather_z_copy(k, d, z_at(16 - d)).wait_recv()

        for d in (2, 1, 3):
            gather_x_copy(k, d, x).start()
        gather_core_copy(k, 0, c).start()
        for d in (1, 3, 2):
            gather_x_copy(k, d, x_at(4 - d)).wait_recv()
            gather_core_copy(k, d, c).start()
        for d in (0, 1, 3, 2):
            gather_core_copy(k, d, 1 - c).wait_recv()

    for d in (2, 1, 3):
        grad_copy(d, 1 - c, y).start()
    for d in (2, 1, 3):
        grad_copy(d, c, y).start()

    @pl.loop(1, 8)
    def _(d):
        lo_copy(1, d, t).start()

    @pl.loop(1, 8)
    def _(d):
        lo_copy(0, d, t).start()

    for d in (2, 1, 3):
        weight_copy(0, d, y).start()

    own[0].wait()
    own[1].wait()
    own[2].wait()
    for d in (1, 3, 2):
        grad_copy(d, 1 - c, y_at(4 - d)).wait_recv()
    half = lax.dot_general(
        gall[1 - c].reshape(256, 512), kvv[...], NT, preferred_element_type=F32
    )
    usend[...] = half.astype(BF16).reshape(4, 64, 1024)
    ucore = remote(usend, crecv, rcsem, (0,), core_dev)
    ucore.start()
    for d in (1, 3, 2):
        grad_copy(d, c, y_at(4 - d)).wait_recv()
    uown[...] = lax.dot_general(
        gall[c].reshape(256, 512), kvv[...], NT, preferred_element_type=F32
    ).reshape(4, 64, 1024)
    ucore.wait_recv()
    for r in range(4):
        xsend[r] = (uown[r] + crecv[r].astype(F32)).astype(BF16)

    def ux_copy(d):
        return remote(xsend.at[:, at(x_at(d), 16), :], xrecv.at[d], rxsem, (0, d), x_dev(d))

    for d in (2, 1, 3):
        ux_copy(d).start()

    own[3].wait()
    own[4].wait()

    @pl.loop(1, 8)
    def _(d):
        lo_copy(1, d, lax.rem(t + 8 - d, 8)).wait_recv()

    for d in (2, 1, 3):
        enc_y_copy(d, y).start()
    ee[y, rows, :] = eb[:, at(y, 1024)]

    @pl.loop(1, 8)
    def _(d):
        lo_copy(0, d, lax.rem(t + 8 - d, 8)).wait_recv()

    for d in (1, 3, 2):
        ux_copy(d).wait_recv()
    for r in range(4):
        total = uown[r, xrows, :] + crecv[r, xrows, :].astype(F32)
        for d in range(1, 4):
            total = total + xrecv[d, r].astype(F32)
        ysend[r] = total.astype(BF16)

    def uy_copy(d, block):
        return remote(ysend.at[y_at(d)], yb.at[:, at(block, 1024)], rysem, (d,), y_dev(d))

    for d in (2, 1, 3):
        uy_copy(d, y).start()
    yb[:, at(y, 1024)] = ysend[y]

    for d in (1, 3, 2):
        enc_y_copy(d, y_at(4 - d)).wait_recv()
    for k in (0, 1):
        for d in (2, 1, 3):
            side_x_copy(k, d, x).start()
    for d in (1, 3, 2):
        uy_copy(d, y_at(4 - d)).wait_recv()

    def uz_copy(d):
        return remote(yb.at[:, at(z_at(d), 256)], zrecv.at[d], rzsem, (0, d), z_dev(d))

    @pl.loop(0, 15)
    def _(i):
        uz_copy(farthest_first(i)).start()

    for k in (1, 2):
        for d in (2, 1, 3):
            weight_copy(k, d, y).start()

    for k in (0, 1):
        for d in (1, 3, 2):
            side_x_copy(k, d, x_at(4 - d)).wait_recv()
        side_core_copy(k, c).start()

    @pl.loop(1, 16)
    def _(d):
        uz_copy(d).wait_recv()

    total = yb[:, at(z, 256)].astype(F32)
    for d in range(1, 16):
        total = total + zrecv[d].astype(F32)
    upf[...] = total
    ub[rows, at(z, 256)] = total.astype(BF16)

    def meanwhile():
        side_core_copy(0, 1 - c).wait_recv()

        @pl.loop(0, 8)
        def _(i):
            r = at(i, 16)
            values = xb[r, :].astype(F32)
            scale = lax.rsqrt(jnp.mean(values * values, axis=1, keepdims=True) + 1e-06)
            nb[r, :] = (values * scale * gain[...].astype(F32)).astype(BF16)
            rsb[r, :] = jnp.broadcast_to(scale, (16, 128))

        own[5].wait()
        own[6].wait()
        for k in (0, 1):
            for d in (1, 3, 2):
                weight_copy(k, d, y_at(4 - d)).wait_recv()
        pre[...] = jnp.dot(nb[...], gu[...], preferred_element_type=F32)
        value, slope = gelu_parts(pre[:, 0:128])
        act[:, 0:128] = pre[:, 128:256] * slope
        act[:, 128:256] = value
        side_core_copy(1, 1 - c).wait_recv()

        @pl.loop(0, 4)
        def _(i):
            total = jnp.zeros((256, 512), F32)
            for r in range(4):
                g_r = jnp.concatenate([gall[0, r], gall[1, r]], axis=0)
                term = lax.dot_general(ee[r, :, at(i, 256)], g_r, TN, preferred_element_type=F32)
                total = total + term.astype(BF16).astype(F32)
            kvg[at(i, 256), :] = total.astype(BF16)

        own[7].wait()
        for d in (1, 3, 2):
            weight_copy(2, d, y_at(4 - d)).wait_recv()

    gather(0, meanwhile)

    hidden = lax.dot_general(ub[...], db[...], NT, preferred_element_type=F32)
    grads = (jnp.concatenate([hidden, hidden], axis=1) * act[...]).astype(BF16)
    gg[...] = grads
    act[...] = jnp.broadcast_to(
        jnp.sum(grads.astype(F32) * pre[...], axis=1, keepdims=True), (128, 256)
    )

    def term(half, block):
        return lax.dot_general(
            gg[at(half, 64), :], gu[pl.ds(block * 1024, 1024), :], NT, preferred_element_type=F32
        )

    for block in range(4):
        psend[:, pl.ds(block * 1024, 1024)] = term(1 - c, block).astype(BF16)
    psend[:, 4096:4224] = act[at(1 - c, 64), 0:128].astype(BF16)
    pcore = remote(psend, pcrecv, rcsem, (1,), core_dev)
    pcore.start()
    for block in range(4):
        pown[:, pl.ds(block * 1024, 1024)] = term(c, block)
    pown[:, 4096:4224] = act[at(c, 64), 0:128]
    pcore.wait_recv()
    for i in range(4):
        r = pl.ds(i * 16, 16)
        pxsend[r, :] = (pown[r, :] + pcrecv[r, :].astype(F32)).astype(BF16)

    def px_copy(d):
        return remote(pxsend.at[at(x_at(d), 16), :], pxrecv.at[d], rxsem, (1, d), x_dev(d))

    for d in (2, 1, 3):
        px_copy(d).start()
    for d in (1, 3, 2):
        px_copy(d).wait_recv()

    def px_sum(columns):
        total = pown[xrows, columns] + pcrecv[xrows, columns].astype(F32)
        for d in range(1, 4):
            total = total + pxrecv[d, :, columns].astype(F32)
        return total.astype(BF16)

    stat = px_sum(pl.ds(4096, 128))
    for i in range(16):
        pzsend[i, :, 0:256] = px_sum(pl.ds(i * 256, 256))
        pzsend[i, :, 256:384] = stat

    def pz_copy(d):
        return remote(pzsend.at[z_at(d)], pzrecv.at[d], rzsem, (1, d), z_dev(d))

    @pl.loop(0, 15)
    def _(i):
        pz_copy(farthest_first(i)).start()

    @pl.loop(1, 16)
    def _(d):
        pz_copy(d).wait_recv()

    total = pzsend[z].astype(F32)
    for d in range(1, 16):
        total = total + pzrecv[d].astype(F32)
    scale = rsb[rows, 0:1]
    values = xb[rows, at(z, 256)].astype(F32)
    gain_here = gain[:, at(z, 256)].astype(F32)
    result = (
        upf[...]
        + scale * gain_here * total[:, 0:256]
        - values * (scale * scale) * (total[:, 256:257] * (1.0 / 4096.0))
    )
    out[rows, at(z, 256)] = result.astype(BF16)
    gather(1)

    for d in range(1, 4):
        for h in (0, 1):
            grad_copy(d, h, y).wait_send()
        for k in range(3):
            weight_copy(k, d, y).wait_send()
        enc_y_copy(d, y).wait_send()
        for k in (0, 1):
            side_x_copy(k, d, x).wait_send()
            gather_x_copy(k, d, x).wait_send()
        ux_copy(d).wait_send()
        uy_copy(d, y).wait_send()
        px_copy(d).wait_send()
    for k in (0, 1):
        side_core_copy(k, c).wait_send()
        for d in range(4):
            gather_core_copy(k, d, c).wait_send()
    ucore.wait_send()
    pcore.wait_send()

    @pl.loop(1, 8)
    def _(d):
        lo_copy(0, d, t).wait_send()
        lo_copy(1, d, t).wait_send()

    @pl.loop(1, 16)
    def _(d):
        uz_copy(d).wait_send()
        pz_copy(d).wait_send()
        gather_z_copy(0, d, z).wait_send()
        gather_z_copy(1, d, z).wait_send()


def on_device(
    enc_out, mlp_input, grad_kv, kv_weight, gate_weight, up_weight, down_weight, norm_gain
):
    vmem = pl.BlockSpec(memory_space=pltpu.VMEM)
    anywhere = pl.BlockSpec(memory_space=pl.ANY)
    dma = pltpu.SemaphoreType.DMA
    input_grad, kv_grad = pl.pallas_call(
        kernel,
        out_shape=(
            jax.ShapeDtypeStruct((128, 4096), BF16),
            jax.ShapeDtypeStruct((1024, 512), BF16),
        ),
        in_specs=[anywhere] * 7 + [vmem],
        out_specs=(vmem, vmem),
        scratch_shapes=[
            pltpu.VMEM((2, 4, 64, 512), BF16),
            pltpu.VMEM((1024, 512), BF16),
            pltpu.VMEM((4, 64, 1024), BF16),
            pltpu.VMEM((4, 64, 1024), F32),
            pltpu.VMEM((4, 64, 1024), BF16),
            pltpu.VMEM((4, 64, 1024), BF16),
            pltpu.VMEM((4, 4, 16, 1024), BF16),
            pltpu.VMEM((4, 16, 1024), BF16),
            pltpu.VMEM((16, 4096), BF16),
            pltpu.VMEM((16, 16, 256), BF16),
            pltpu.VMEM((16, 256), F32),
            pltpu.VMEM((128, 4096), BF16),
            pltpu.VMEM((4096, 256), BF16),
            pltpu.VMEM((128, 4096), BF16),
            pltpu.VMEM((128, 4096), BF16),
            pltpu.VMEM((128, 4096), BF16),
            pltpu.VMEM((128, 128), F32),
            pltpu.VMEM((16, 4096), BF16),
            pltpu.VMEM((4, 128, 1024), BF16),
            pltpu.VMEM((128, 256), F32),
            pltpu.VMEM((128, 256), F32),
            pltpu.VMEM((128, 256), BF16),
            pltpu.VMEM((64, 4224), BF16),
            pltpu.VMEM((64, 4224), F32),
            pltpu.VMEM((64, 4224), BF16),
            pltpu.VMEM((64, 4224), BF16),
            pltpu.VMEM((4, 16, 4224), BF16),
            pltpu.VMEM((16, 16, 384), BF16),
            pltpu.VMEM((16, 16, 384), BF16),
            dma((8,)),
            dma((2, 4, 2)),
            dma((2, 3, 4)),
            dma((2, 2, 8)),
            dma((2, 4)),
            dma((2, 2, 4)),
            dma((2, 2)),
            dma((2, 2)),
            dma((2, 2, 4)),
            dma((2, 4)),
            dma((2, 2, 16)),
            dma((2, 2, 16)),
            dma((2, 2, 4)),
            dma((2, 2, 4)),
        ],
        compiler_params=pltpu.CompilerParams(collective_id=0, has_side_effects=True),
    )(
        enc_out,
        mlp_input,
        grad_kv.reshape(128, 512),
        kv_weight.reshape(1024, 512),
        gate_weight,
        up_weight,
        down_weight,
        norm_gain.reshape(1, 4096),
    )
    return (input_grad, kv_grad.reshape(1024, 2, 1, 256))


def solution(mesh):
    placed = (
        P("dp", "tensor"),
        P("dp", "tensor"),
        P("dp", None, "pipe", "tensor"),
        P("dp", None, "pipe", "tensor"),
        P("dp", ("pipe", "tensor")),
        P("dp", ("pipe", "tensor")),
        P(("pipe", "tensor"), "dp"),
        P(),
    )
    return jax.shard_map(
        on_device,
        mesh=mesh,
        in_specs=placed,
        out_specs=(P("dp", None), P("dp", None, "pipe", "tensor")),
        check_vma=False,
    )
```

time: 1070 us -> 123 us (0.11)
  waiting for transfers between devices: 1030 us -> 0 us
  Pallas kernels: 0 us -> 114 us
  matrix products: 19.3 us -> 0 us
  between operations: 13.9 us -> 0.65 us
    psum x2 -> x0, waiting for transfers between devices: 706 us -> none  [the longest x1 356 us: on_device(): upstream = lax.psum(partial_value, ('pipe', 'tensor'))]
    all_gather x6 -> x0, waiting for transfers between devices: 268 us -> none  [the longest x1 60.3 us: on_device(): lax.all_gather(enc_out, 'tensor', axis=1, tiled=True)]
    pallas_call x0 -> x1, Pallas kernels: none -> 114 us  [on_device(): pl.pallas_call(kernel, out_shape=(jax.ShapeDtypeStruct((128, 4096), BF16)...]
    reduce_scatter x1 -> x0, waiting for transfers between devices: 50.7 us -> none  [on_device(): lax.psum_scatter(jnp.einsum('td,tslc->dslc', encoded, grad_kv, preferred_...]
    dot_general x6 -> x0, matrix products: 19.3 us -> none  [the longest x1 5.02 us: on_device(): jnp.einsum('tslc,dslc->td', grad_kv, lax.all_gather(kv_weight, 'dp', axis...]
  transfers between devices with their start and end apart: 9 -> 0, of which waited for: 9 -> 0; matrix products, arithmetic and copies ran while one was open for 2% -> 0% of each run, Pallas kernels for 0% -> 0%
where the time goes in v1:
time: 123 us
  Pallas kernels  114 us (93%)
  local copies, waits for them, and re-layouts  8.5 us (7%)
    pallas_call x1, Pallas kernels, on_device(): pl.pallas_call(kernel, out_shape=(jax.ShapeDtypeStruct((128, 4096), BF16)...  114 us
    unnamed x5, local copies, waits for them, and re-layouts  4.97 us

profile of v1, /device:TPU:1, one launch (start us, length us, event | category | flops | bytes accessed | tf_op | source)
XLA Modules:
  0.0 122.8 jit_solution(16619209351540062020)
XLA Ops:
  0.6 1.3 %reshape.18.gain = bf16[1,4096]{1,0:T(2,128)(2,1)} reshape(bf16[4096]{0:T(1024)(128)(2,1)} %param.15) | data formatting | bytes 16384 | tf_op jit(solution)/shard_map/reshape | solution.py:488
  1.9 1.6 %copy.11 = bf16[16,8,2,256]{3,1,2,0:T(8,128)(2,1)} copy(bf16[16,8,2,256]{3,2,1,0:T(2,128)(2,1)} %bitcast.13) | data formatting | bytes 262144
  3.5 2.4 %copy.12 = bf16[128,8,2,256]{3,1,2,0:T(8,128)(2,1)} copy(bf16[128,8,2,256]{3,2,1,0:T(2,128)(2,1)} %bitcast.10) | data formatting | bytes 2097152
  5.9 113.6 %shard_map.95 = (bf16[128,4096]{1,0:T(8,128)(2,1)}, bf16[1024,512]{1,0:T(8,128)(2,1)}) custom-call(bf16[128,512]{1,0:T(8,128)(2,1)} %enc.1, bf16[128,512]{1,0:T(8,128)(2,1)} %mlp.1, bf16[128,512]{1,0:T(8,128)(2,1)} %bitcast.12, bf16[1024,512]{1,0:T(8,128)(2,1)} %bitcast.9, bf16[1024,128]{1,0:T(8,128)(2,1)} %gate.1, bf16[1024,128]{1,0:T(8,128)(2,1)} %up.1, ...), custom_call_target="tpu_custom_call" | custom-call | tf_op jit(solution)/shard_map/pallas_call | solution.py:426
  119.5 0.0 copy-start
  119.6 2.2 %reshape.19 = bf16[1024,2,1,256]{3,1,0,2:T(2,128)(2,1)} reshape(bf16[1024,512]{1,0:T(8,128)(2,1)} %get-tuple-element.5) | data formatting | bytes 2097152 | tf_op jit(solution)/shard_map/reshape | solution.py:490
  121.8 0.0 copy-done
  121.8 1.0 copy.14
Async XLA Ops:
  119.5 2.2 %copy-start = (bf16[128,4096]{1,0:T(8,128)(2,1)S(1)}, bf16[128,4096]{1,0:T(8,128)(2,1)}, u32[]{:S(2)}) copy-start(bf16[128,4096]{1,0:T(8,128)(2,1)} %get-tuple-element.10) | copy-start | bytes 3145732

commit v2 on v1

--- a/solution.py
+++ b/solution.py
@@ -29,9 +29,10 @@
 
 def kernel(
     enc, mlp, grad, kvw, gate, up, down, gain, out, kvg,
-    gall, kvv, usend, uown, crecv, xsend, xrecv, ysend, yb, zrecv, upf, ub,
-    gu, db, xb, nb, rsb, eb, ee, act, pre, gg, psend, pown, pcrecv, pxsend, pxrecv, pzsend, pzrecv,
-    lsem, gsem, wsem, msem, esem, mxsem, mcsem, rcsem, rxsem, rysem, rzsem, azsem, axsem, acsem,
+    gin, kin, gall, kvv, usend, uown, crecv, xsend, xrecv, ysend, yb, zrecv, upf, ub,
+    gu, db, xb, nb, rsb, gf, eb, ee, act, pre, gg, psend, pown, pcrecv, pxsend, pxrecv, pzsend, pzrecv,
+    szrecv, sxsend, sxrecv, scsend, screcv, left, right,
+    lsem, gsem, wsem, msem, esem, mxsem, mcsem, rcsem, rxsem, rysem, rzsem, azsem, axsem, acsem, szsem, sxsem, scsem,
 ):
     y, pipe, t = lax.axis_index("dp"), lax.axis_index("pipe"), lax.axis_index("tensor")
     zh, x, c = lax.div(pipe, 8), lax.rem(lax.div(pipe, 2), 4), lax.rem(pipe, 2)
@@ -75,42 +76,61 @@
     def greet(device):
         pl.semaphore_signal(barrier, inc=1, device_id=device, device_id_type=MESH)
 
-    @pl.loop(1, 16)
-    def _(d):
-        greet(z_dev(d))
-
-    @pl.loop(1, 4)
-    def _(d):
+    for d in (1, 2, 3):
         greet(y_dev(d))
         greet(x_dev(d))
-
     greet(core_dev)
+    greet(z_dev(1))
+    greet(z_dev(15))
 
     own = [
-        pltpu.make_async_copy(grad.at[at(0, 64)], gall.at[0, y], lsem.at[0]),
-        pltpu.make_async_copy(grad.at[at(1, 64)], gall.at[1, y], lsem.at[1]),
-        pltpu.make_async_copy(kvw, kvv, lsem.at[2]),
-        pltpu.make_async_copy(mlp.at[rows], xb.at[rows, at(t, 512)], lsem.at[3]),
-        pltpu.make_async_copy(enc.at[rows], eb.at[:, at(t, 512)], lsem.at[4]),
-        pltpu.make_async_copy(gate, gu.at[at(y, 1024), pl.ds(0, 128)], lsem.at[5]),
-        pltpu.make_async_copy(up, gu.at[at(y, 1024), pl.ds(128, 128)], lsem.at[6]),
-        pltpu.make_async_copy(down, db.at[:, at(y, 1024)], lsem.at[7]),
+        pltpu.make_async_copy(grad, gin, lsem.at[0]),
+        pltpu.make_async_copy(kvw, kin, lsem.at[1]),
+        pltpu.make_async_copy(mlp.at[rows], xb.at[rows, at(t, 512)], lsem.at[2]),
+        pltpu.make_async_copy(enc.at[rows], eb.at[:, at(t, 512)], lsem.at[3]),
+        pltpu.make_async_copy(gate, gu.at[at(y, 1024), pl.ds(0, 128)], lsem.at[4]),
+        pltpu.make_async_copy(up, gu.at[at(y, 1024), pl.ds(128, 128)], lsem.at[5]),
+        pltpu.make_async_copy(down, db.at[:, at(y, 1024)], lsem.at[6]),
     ]
     for copy in own:
         copy.start()
-
-    pl.semaphore_wait(barrier, 22)
+    own[0].wait()
+    for h in range(2):
+        for k in range(2):
+            gall[h, y, :, pl.ds(k * 256, 256)] = gin[pl.ds(h * 64, 64), k, :]
+
+    pl.semaphore_wait(barrier, 9)
 
     def grad_copy(d, h, to):
-        return remote(grad.at[at(h, 64)], gall.at[h, to], gsem, (d, h), y_dev(d))
-
-    def weight_copy(k, d, block):
-        src, dst = (
-            (gate, gu.at[at(block, 1024), pl.ds(0, 128)]),
-            (up, gu.at[at(block, 1024), pl.ds(128, 128)]),
-            (down, db.at[:, at(block, 1024)]),
+        return remote(gall.at[h, y], gall.at[h, to], gsem, (d, h), y_dev(d))
+
+    def weight_part(k, block, p):
+        return (
+            gu.at[pl.ds(pl.multiple_of(block * 1024 + p * 512, 512), 512), pl.ds(0, 128)],
+            gu.at[pl.ds(pl.multiple_of(block * 1024 + p * 512, 512), 512), pl.ds(128, 128)],
+            db.at[:, pl.ds(pl.multiple_of(block * 1024 + p * 512, 512), 512)],
         )[k]
-        return remote(src, dst, wsem, (k, d), y_dev(d))
+
+    def near_copy(k, way, p, block):
+        half = pl.ds(p * 512, 512)
+        src = (gate.at[half, :], up.at[half, :], down.at[:, half])[k]
+        return remote(src, weight_part(k, block, p), wsem, (k, way, p), y_dev(1 + 2 * way))
+
+    def far_copy(k, p):
+        part = weight_part(k, y_at(3 - 2 * p), p)
+        return remote(part, part, wsem, (k, 2, p), y_dev(1 + 2 * p))
+
+    def relay(k):
+        for p in (0, 1):
+            near_copy(k, p, p, y_at(3 - 2 * p)).wait_recv()
+            far_copy(k, p).start()
+
+    def weight_here(k):
+        own[4 + k].wait()
+        for p in (0, 1):
+            near_copy(k, 1 - p, p, y_at(1 + 2 * p)).wait_recv()
+            part = weight_part(k, y_at(2), p)
+            remote(part, part, wsem, (k, 2, p), y_dev(1 + 2 * p)).wait_recv()
 
     def lo_copy(k, d, block):
         src = (mlp, enc)[k].at[rows]
@@ -151,14 +171,14 @@
         j = lax.div(k + 1, 2)
         return 8 + j * (1 - 2 * lax.rem(k, 2))
 
-    def gather(k, before_rows=None):
+    def gather(k, under_z=None, under_x=None):
         @pl.loop(0, 15)
         def _(i):
             d = farthest_first(i)
             gather_z_copy(k, d, z).start()
 
-        if before_rows is not None:
-            before_rows()
+        if under_z is not None:
+            under_z()
 
         @pl.loop(1, 16)
         def _(d):
@@ -167,31 +187,39 @@
         for d in (2, 1, 3):
             gather_x_copy(k, d, x).start()
         gather_core_copy(k, 0, c).start()
+        if under_x is not None:
+            under_x()
         for d in (1, 3, 2):
             gather_x_copy(k, d, x_at(4 - d)).wait_recv()
             gather_core_copy(k, d, c).start()
         for d in (0, 1, 3, 2):
             gather_core_copy(k, d, 1 - c).wait_recv()
 
+    def tell(i):
+        pl.semaphore_signal(left.at[i], inc=1, device_id=z_dev(2**i), device_id_type=MESH)
+        pl.semaphore_signal(right.at[i], inc=1, device_id=z_dev(16 - 2**i), device_id_type=MESH)
+
+    def heard(i):
+        pl.semaphore_wait(left.at[i], 1)
+        pl.semaphore_wait(right.at[i], 1)
+
+    tell(0)
+
     for d in (2, 1, 3):
         grad_copy(d, 1 - c, y).start()
     for d in (2, 1, 3):
         grad_copy(d, c, y).start()
 
-    @pl.loop(1, 8)
-    def _(d):
-        lo_copy(1, d, t).start()
-
-    @pl.loop(1, 8)
-    def _(d):
-        lo_copy(0, d, t).start()
-
-    for d in (2, 1, 3):
-        weight_copy(0, d, y).start()
-
-    own[0].wait()
     own[1].wait()
-    own[2].wait()
+
+    @pl.loop(0, 8)
+    def _(i):
+        r = at(i, 128)
+        for k in range(2):
+            kvv[r, pl.ds(k * 256, 256)] = kin[r, k, :]
+
+    heard(0)
+    tell(1)
     for d in (1, 3, 2):
         grad_copy(d, 1 - c, y_at(4 - d)).wait_recv()
     half = lax.dot_general(
@@ -200,8 +228,12 @@
     usend[...] = half.astype(BF16).reshape(4, 64, 1024)
     ucore = remote(usend, crecv, rcsem, (0,), core_dev)
     ucore.start()
+    heard(1)
+    tell(2)
     for d in (1, 3, 2):
         grad_copy(d, c, y_at(4 - d)).wait_recv()
+    for k, way, p in ((0, 0, 0), (0, 1, 1), (0, 0, 1), (0, 1, 0), (1, 0, 0), (1, 1, 1)):
+        near_copy(k, way, p, y).start()
     uown[...] = lax.dot_general(
         gall[c].reshape(256, 512), kvv[...], NT, preferred_element_type=F32
     ).reshape(4, 64, 1024)
@@ -214,21 +246,16 @@
 
     for d in (2, 1, 3):
         ux_copy(d).start()
-
-    own[3].wait()
-    own[4].wait()
+    heard(2)
 
     @pl.loop(1, 8)
     def _(d):
-        lo_copy(1, d, lax.rem(t + 8 - d, 8)).wait_recv()
-
-    for d in (2, 1, 3):
-        enc_y_copy(d, y).start()
-    ee[y, rows, :] = eb[:, at(y, 1024)]
+        lo_copy(0, d, t).start()
 
     @pl.loop(1, 8)
     def _(d):
-        lo_copy(0, d, lax.rem(t + 8 - d, 8)).wait_recv()
+        lo_copy(1, d, t).start()
+
 
     for d in (1, 3, 2):
         ux_copy(d).wait_recv()
@@ -244,12 +271,11 @@
     for d in (2, 1, 3):
         uy_copy(d, y).start()
     yb[:, at(y, 1024)] = ysend[y]
-
-    for d in (1, 3, 2):
-        enc_y_copy(d, y_at(4 - d)).wait_recv()
-    for k in (0, 1):
-        for d in (2, 1, 3):
-            side_x_copy(k, d, x).start()
+    relay(0)
+    relay(1)
+    for k, way, p in ((1, 0, 1), (1, 1, 0), (2, 0, 0), (2, 1, 1), (2, 0, 1), (2, 1, 0)):
+        near_copy(k, way, p, y).start()
+
     for d in (1, 3, 2):
         uy_copy(d, y_at(4 - d)).wait_recv()
 
@@ -260,14 +286,23 @@
     def _(i):
         uz_copy(farthest_first(i)).start()
 
-    for k in (1, 2):
-        for d in (2, 1, 3):
-            weight_copy(k, d, y).start()
-
-    for k in (0, 1):
-        for d in (1, 3, 2):
-            side_x_copy(k, d, x_at(4 - d)).wait_recv()
-        side_core_copy(k, c).start()
+    own[2].wait()
+
+    @pl.loop(1, 8)
+    def _(d):
+        lo_copy(0, d, lax.rem(t + 8 - d, 8)).wait_recv()
+
+    for d in (2, 1, 3):
+        side_x_copy(0, d, x).start()
+    own[3].wait()
+
+    @pl.loop(1, 8)
+    def _(d):
+        lo_copy(1, d, lax.rem(t + 8 - d, 8)).wait_recv()
+
+    for d in (2, 1, 3):
+        enc_y_copy(d, y).start()
+    ee[y, rows, :] = eb[:, at(y, 1024)]
 
     @pl.loop(1, 16)
     def _(d):
@@ -279,26 +314,35 @@
     upf[...] = total
     ub[rows, at(z, 256)] = total.astype(BF16)
 
-    def meanwhile():
+    def normalize():
+        relay(2)
+        for d in (1, 3, 2):
+            side_x_copy(0, d, x_at(4 - d)).wait_recv()
+        side_core_copy(0, c).start()
         side_core_copy(0, 1 - c).wait_recv()
+        gf[...] = gain[...].astype(F32)
 
         @pl.loop(0, 8)
         def _(i):
             r = at(i, 16)
             values = xb[r, :].astype(F32)
             scale = lax.rsqrt(jnp.mean(values * values, axis=1, keepdims=True) + 1e-06)
-            nb[r, :] = (values * scale * gain[...].astype(F32)).astype(BF16)
             rsb[r, :] = jnp.broadcast_to(scale, (16, 128))
 
-        own[5].wait()
-        own[6].wait()
-        for k in (0, 1):
-            for d in (1, 3, 2):
-                weight_copy(k, d, y_at(4 - d)).wait_recv()
+        for j in range(32):
+            columns = pl.ds(j * 128, 128)
+            values = xb[:, columns].astype(F32) * rsb[...]
+            nb[:, columns] = (values * gf[j : j + 1, :]).astype(BF16)
+
+    def hidden_units():
+        weight_here(0)
+        weight_here(1)
         pre[...] = jnp.dot(nb[...], gu[...], preferred_element_type=F32)
         value, slope = gelu_parts(pre[:, 0:128])
         act[:, 0:128] = pre[:, 128:256] * slope
         act[:, 128:256] = value
+
+    def kv_rows():
         side_core_copy(1, 1 - c).wait_recv()
 
         @pl.loop(0, 4)
@@ -308,21 +352,16 @@
                 g_r = jnp.concatenate([gall[0, r], gall[1, r]], axis=0)
                 term = lax.dot_general(ee[r, :, at(i, 256)], g_r, TN, preferred_element_type=F32)
                 total = total + term.astype(BF16).astype(F32)
-            kvg[at(i, 256), :] = total.astype(BF16)
-
-        own[7].wait()
-        for d in (1, 3, 2):
-            weight_copy(2, d, y_at(4 - d)).wait_recv()
-
-    gather(0, meanwhile)
-
+            total = total.astype(BF16)
+            for k in range(2):
+                kvg[at(i, 256), k, :] = total[:, k * 256 : k * 256 + 256]
+
+    gather(0, normalize, hidden_units)
+
+    weight_here(2)
     hidden = lax.dot_general(ub[...], db[...], NT, preferred_element_type=F32)
     grads = (jnp.concatenate([hidden, hidden], axis=1) * act[...]).astype(BF16)
     gg[...] = grads
-    act[...] = jnp.broadcast_to(
-        jnp.sum(grads.astype(F32) * pre[...], axis=1, keepdims=True), (128, 256)
-    )
-
     def term(half, block):
         return lax.dot_general(
             gg[at(half, 64), :], gu[pl.ds(block * 1024, 1024), :], NT, preferred_element_type=F32
@@ -330,12 +369,31 @@
 
     for block in range(4):
         psend[:, pl.ds(block * 1024, 1024)] = term(1 - c, block).astype(BF16)
-    psend[:, 4096:4224] = act[at(1 - c, 64), 0:128].astype(BF16)
     pcore = remote(psend, pcrecv, rcsem, (1,), core_dev)
     pcore.start()
     for block in range(4):
         pown[:, pl.ds(block * 1024, 1024)] = term(c, block)
-    pown[:, 4096:4224] = act[at(c, 64), 0:128]
+
+    product = gg[...].astype(F32) * pre[...]
+    high = product.astype(BF16)
+    low = (product - high.astype(F32)).astype(BF16)
+    ones = jnp.ones((8, 256), BF16)
+    szrecv[0] = lax.dot_general(ones, high, NT, preferred_element_type=F32) + lax.dot_general(
+        ones, low, NT, preferred_element_type=F32
+    )
+
+    def sz_copy(d):
+        return remote(szrecv.at[0], szrecv.at[d], szsem, (d,), z_dev(d))
+
+    def sx_copy(d):
+        return remote(sxsend, sxrecv.at[d], sxsem, (d,), x_dev(d))
+
+    score = remote(scsend, screcv, scsem, (), core_dev)
+
+    @pl.loop(0, 15)
+    def _(i):
+        sz_copy(farthest_first(i)).start()
+
     pcore.wait_recv()
     for i in range(4):
         r = pl.ds(i * 16, 16)
@@ -346,50 +404,66 @@
 
     for d in (2, 1, 3):
         px_copy(d).start()
+    @pl.loop(1, 16)
+    def _(d):
+        sz_copy(d).wait_recv()
+
+    total = szrecv[0]
+    for d in range(1, 16):
+        total = total + szrecv[d]
+    sxsend[...] = total
+    for d in (2, 1, 3):
+        sx_copy(d).start()
     for d in (1, 3, 2):
         px_copy(d).wait_recv()
-
-    def px_sum(columns):
+    for i in range(4):
+        columns = pl.ds(i * 1024, 1024)
         total = pown[xrows, columns] + pcrecv[xrows, columns].astype(F32)
         for d in range(1, 4):
             total = total + pxrecv[d, :, columns].astype(F32)
-        return total.astype(BF16)
-
-    stat = px_sum(pl.ds(4096, 128))
-    for i in range(16):
-        pzsend[i, :, 0:256] = px_sum(pl.ds(i * 256, 256))
-        pzsend[i, :, 256:384] = stat
+        pzsend[:, columns] = total.astype(BF16)
 
     def pz_copy(d):
-        return remote(pzsend.at[z_at(d)], pzrecv.at[d], rzsem, (1, d), z_dev(d))
+        return remote(pzsend.at[:, at(z_at(d), 256)], pzrecv.at[d], rzsem, (1, d), z_dev(d))
 
     @pl.loop(0, 15)
     def _(i):
         pz_copy(farthest_first(i)).start()
 
+    for d in (1, 3, 2):
+        enc_y_copy(d, y_at(4 - d)).wait_recv()
+    for d in (2, 1, 3):
+        side_x_copy(1, d, x).start()
+    for d in (1, 3, 2):
+        sx_copy(d).wait_recv()
+    scsend[...] = sxsend[...] + sxrecv[1] + sxrecv[2] + sxrecv[3]
+    score.start()
+    score.wait_recv()
+    stat_row = scsend[0:1, :] + screcv[0:1, :]
+    token = c * 64 + x * 16 + lax.broadcasted_iota(jnp.int32, (16, 128), 0)
+    mine = lax.broadcasted_iota(jnp.int32, (16, 128), 1) == token
+    stat = jnp.sum(jnp.where(mine, jnp.broadcast_to(stat_row, (16, 128)), 0.0), axis=1, keepdims=True)
+    scale = rsb[rows, 0:1]
+    values = xb[rows, at(z, 256)].astype(F32)
+    gain_here = jnp.concatenate([gf[pl.ds(2 * z, 1), :], gf[pl.ds(2 * z + 1, 1), :]], axis=1)
+    base = upf[...] - values * (scale * scale) * (stat * (1.0 / 4096.0))
+
     @pl.loop(1, 16)
     def _(d):
         pz_copy(d).wait_recv()
 
-    total = pzsend[z].astype(F32)
+    for d in (1, 3, 2):
+        side_x_copy(1, d, x_at(4 - d)).wait_recv()
+    side_core_copy(1, c).start()
+    total = pzsend[:, at(z, 256)].astype(F32)
     for d in range(1, 16):
         total = total + pzrecv[d].astype(F32)
-    scale = rsb[rows, 0:1]
-    values = xb[rows, at(z, 256)].astype(F32)
-    gain_here = gain[:, at(z, 256)].astype(F32)
-    result = (
-        upf[...]
-        + scale * gain_here * total[:, 0:256]
-        - values * (scale * scale) * (total[:, 256:257] * (1.0 / 4096.0))
-    )
-    out[rows, at(z, 256)] = result.astype(BF16)
-    gather(1)
+    out[rows, at(z, 256)] = (base + scale * gain_here * total).astype(BF16)
+    gather(1, kv_rows)
 
     for d in range(1, 4):
         for h in (0, 1):
             grad_copy(d, h, y).wait_send()
-        for k in range(3):
-            weight_copy(k, d, y).wait_send()
         enc_y_copy(d, y).wait_send()
         for k in (0, 1):
             side_x_copy(k, d, x).wait_send()
@@ -397,11 +471,18 @@
         ux_copy(d).wait_send()
         uy_copy(d, y).wait_send()
         px_copy(d).wait_send()
+        sx_copy(d).wait_send()
     for k in (0, 1):
         side_core_copy(k, c).wait_send()
         for d in range(4):
             gather_core_copy(k, d, c).wait_send()
+    for k in range(3):
+        for p in (0, 1):
+            near_copy(k, 0, p, y).wait_send()
+            near_copy(k, 1, p, y).wait_send()
+            far_copy(k, p).wait_send()
     ucore.wait_send()
+    score.wait_send()
     pcore.wait_send()
 
     @pl.loop(1, 8)
@@ -413,6 +494,7 @@
     def _(d):
         uz_copy(d).wait_send()
         pz_copy(d).wait_send()
+        sz_copy(d).wait_send()
         gather_z_copy(0, d, z).wait_send()
         gather_z_copy(1, d, z).wait_send()
 
@@ -427,11 +509,13 @@
         kernel,
         out_shape=(
             jax.ShapeDtypeStruct((128, 4096), BF16),
-            jax.ShapeDtypeStruct((1024, 512), BF16),
+            jax.ShapeDtypeStruct((1024, 2, 256), BF16),
         ),
         in_specs=[anywhere] * 7 + [vmem],
         out_specs=(vmem, vmem),
         scratch_shapes=[
+            pltpu.VMEM((128, 2, 256), BF16),
+            pltpu.VMEM((1024, 2, 256), BF16),
             pltpu.VMEM((2, 4, 64, 512), BF16),
             pltpu.VMEM((1024, 512), BF16),
             pltpu.VMEM((4, 64, 1024), BF16),
@@ -449,21 +533,29 @@
             pltpu.VMEM((128, 4096), BF16),
             pltpu.VMEM((128, 4096), BF16),
             pltpu.VMEM((128, 128), F32),
+            pltpu.VMEM((32, 128), F32),
             pltpu.VMEM((16, 4096), BF16),
             pltpu.VMEM((4, 128, 1024), BF16),
             pltpu.VMEM((128, 256), F32),
             pltpu.VMEM((128, 256), F32),
             pltpu.VMEM((128, 256), BF16),
-            pltpu.VMEM((64, 4224), BF16),
-            pltpu.VMEM((64, 4224), F32),
-            pltpu.VMEM((64, 4224), BF16),
-            pltpu.VMEM((64, 4224), BF16),
-            pltpu.VMEM((4, 16, 4224), BF16),
-            pltpu.VMEM((16, 16, 384), BF16),
-            pltpu.VMEM((16, 16, 384), BF16),
+            pltpu.VMEM((64, 4096), BF16),
+            pltpu.VMEM((64, 4096), F32),
+            pltpu.VMEM((64, 4096), BF16),
+            pltpu.VMEM((64, 4096), BF16),
+            pltpu.VMEM((4, 16, 4096), BF16),
+            pltpu.VMEM((16, 4096), BF16),
+            pltpu.VMEM((16, 16, 256), BF16),
+            pltpu.VMEM((16, 8, 128), F32),
+            pltpu.VMEM((8, 128), F32),
+            pltpu.VMEM((4, 8, 128), F32),
+            pltpu.VMEM((8, 128), F32),
+            pltpu.VMEM((8, 128), F32),
+            pltpu.SemaphoreType.REGULAR((3,)),
+            pltpu.SemaphoreType.REGULAR((3,)),
             dma((8,)),
             dma((2, 4, 2)),
-            dma((2, 3, 4)),
+            dma((2, 3, 3, 2)),
             dma((2, 2, 8)),
             dma((2, 4)),
             dma((2, 2, 4)),
@@ -475,17 +567,20 @@
             dma((2, 2, 16)),
             dma((2, 2, 4)),
             dma((2, 2, 4)),
+            dma((2, 16)),
+            dma((2, 4)),
+            dma((2,)),
         ],
         compiler_params=pltpu.CompilerParams(collective_id=0, has_side_effects=True),
     )(
         enc_out,
         mlp_input,
-        grad_kv.reshape(128, 512),
-        kv_weight.reshape(1024, 512),
+        grad_kv.reshape(128, 2, 256),
+        kv_weight.reshape(1024, 2, 256),
         gate_weight,
         up_weight,
         down_weight,
-        norm_gain.reshape(1, 4096),
+        norm_gain.reshape(32, 128),
     )
     return (input_grad, kv_grad.reshape(1024, 2, 1, 256))
 

time: 123 us -> 104 us (0.85)
  Pallas kernels: 114 us -> 100 us
  local copies, waits for them, and re-layouts: 8.5 us -> 3.35 us
    pallas_call x1, Pallas kernels: 114 us -> 100 us  [on_device(): pl.pallas_call(kernel, out_shape=(jax.ShapeDtypeStruct((128, 4096), BF16)...]
    reshape x2 -> x0, local copies, waits for them, and re-layouts: 3.53 us -> none  [the longest x1 2.22 us: on_device(): return (input_grad, kv_grad.reshape(1024, 2, 1, 256))]
    unnamed x5 -> x4, local copies, waits for them, and re-layouts: 4.97 us -> 3.35 us
where the time goes in v2:
time: 104 us
  Pallas kernels  100 us (96%)
  local copies, waits for them, and re-layouts  3.35 us (3%)
    pallas_call x1, Pallas kernels, on_device(): pl.pallas_call(kernel, out_shape=(jax.ShapeDtypeStruct((128, 4096), BF16)...  100 us
    unnamed x4, local copies, waits for them, and re-layouts  3.35 us

profile of v2, /device:TPU:1, one launch (start us, length us, event | category | flops | bytes accessed | tf_op | source)
XLA Modules:
  0.0 104.1 jit_solution(5658794038694670876)
XLA Ops:
  0.6 100.1 %shard_map.95 = (bf16[128,4096]{1,0:T(8,128)(2,1)}, bf16[1024,2,256]{2,1,0:T(2,128)(2,1)}) custom-call(bf16[128,512]{1,0:T(8,128)(2,1)} %enc.1, bf16[128,512]{1,0:T(8,128)(2,1)} %mlp.1, bf16[128,2,256]{2,1,0:T(2,128)(2,1)} %bitcast.8, bf16[1024,2,256]{2,1,0:T(2,128)(2,1)} %bitcast.6, bf16[1024,128]{1,0:T(8,128)(2,1)} %gate.1, bf16[1024,128]{1,0:T(8,128)(2,1)} %up.1, ...), custom_call_target="tpu_custom_call" | custom-call | tf_op jit(solution)/shard_map/pallas_call | solution.py:508
  100.7 0.0 copy-start
  100.8 2.4 %copy.13 = bf16[128,4096]{1,0:T(8,128)(2,1)} copy(bf16[128,4096]{1,0:T(8,128)(2,1)} %get-tuple-element.10) | data formatting | bytes 2097152
  103.1 0.0 copy-done
  103.1 1.0 copy.14
Async XLA Ops:
  100.7 2.4 %copy-start = (bf16[1024,2,256]{2,1,0:T(2,128)(2,1)S(1)}, bf16[1024,2,256]{2,1,0:T(2,128)(2,1)}, u32[]{:S(2)}) copy-start(bf16[1024,2,256]{2,1,0:T(2,128)(2,1)} %get-tuple-element.5) | copy-start | bytes 3145732

commit v3 on v2

--- a/solution.py
+++ b/solution.py
@@ -30,9 +30,9 @@
 def kernel(
     enc, mlp, grad, kvw, gate, up, down, gain, out, kvg,
     gin, kin, gall, kvv, usend, uown, crecv, xsend, xrecv, ysend, yb, zrecv, upf, ub,
-    gu, db, xb, nb, rsb, gf, eb, ee, act, pre, gg, psend, pown, pcrecv, pxsend, pxrecv, pzsend, pzrecv,
+    gu, db, ob, xb, nb, rsb, gf, eb, ee, act, pre, gg, psend, pown, pcrecv, pxsend, pxrecv, pzsend, pzrecv,
     szrecv, sxsend, sxrecv, scsend, screcv, left, right,
-    lsem, gsem, wsem, msem, esem, mxsem, mcsem, rcsem, rxsem, rysem, rzsem, azsem, axsem, acsem, szsem, sxsem, scsem,
+    lsem, gsem, wsem, msem, esem, mxsem, mcsem, rcsem, rxsem, rysem, rzsem, azsem, axsem, acsem, szsem, sxsem, scsem, osem,
 ):
     y, pipe, t = lax.axis_index("dp"), lax.axis_index("pipe"), lax.axis_index("tensor")
     zh, x, c = lax.div(pipe, 8), lax.rem(lax.div(pipe, 2), 4), lax.rem(pipe, 2)
@@ -90,7 +90,8 @@
         pltpu.make_async_copy(enc.at[rows], eb.at[:, at(t, 512)], lsem.at[3]),
         pltpu.make_async_copy(gate, gu.at[at(y, 1024), pl.ds(0, 128)], lsem.at[4]),
         pltpu.make_async_copy(up, gu.at[at(y, 1024), pl.ds(128, 128)], lsem.at[5]),
-        pltpu.make_async_copy(down, db.at[:, at(y, 1024)], lsem.at[6]),
+        pltpu.make_async_copy(down.at[:, pl.ds(0, 512)], db.at[0, :, at(y, 512)], lsem.at[6]),
+        pltpu.make_async_copy(down.at[:, pl.ds(512, 512)], db.at[1, :, at(y, 512)], lsem.at[7]),
     ]
     for copy in own:
         copy.start()
@@ -108,7 +109,7 @@
         return (
             gu.at[pl.ds(pl.multiple_of(block * 1024 + p * 512, 512), 512), pl.ds(0, 128)],
             gu.at[pl.ds(pl.multiple_of(block * 1024 + p * 512, 512), 512), pl.ds(128, 128)],
-            db.at[:, pl.ds(pl.multiple_of(block * 1024 + p * 512, 512), 512)],
+            db.at[p, :, at(block, 512)],
         )[k]
 
     def near_copy(k, way, p, block):
@@ -151,49 +152,94 @@
         dst = (xb.at[at(half, 64), :], ee.at[:, at(half, 64), :])[k]
         return remote(ref, dst, mcsem, (k,), core_dev)
 
-    def gather_z_copy(k, d, block):
-        ref = (ub, out)[k]
-        return remote(ref.at[rows, at(z, 256)], ref.at[rows, at(block, 256)], azsem, (k, d), z_dev(d))
-
-    def gather_x_copy(k, d, block):
-        ref = (ub, out)[k]
+    def to_core(k, h):
+        src, dst = ((usend, crecv), (psend, pcrecv))[k]
+        return remote(src.at[h], dst.at[h], rcsem, (k, h), core_dev)
+
+    def to_x(k, h, d):
+        if k == 0:
+            return remote(
+                xsend.at[h, :, at(x_at(d), 16), :], xrecv.at[h, d], rxsem, (k, h, d), x_dev(d)
+            )
+        return remote(
+            pxsend.at[h, at(x_at(d), 16), :], pxrecv.at[h, d], rxsem, (k, h, d), x_dev(d)
+        )
+
+    def to_y(h, d, block):
+        return remote(
+            ysend.at[h, y_at(d)], yb.at[h, :, at(block, 512)], rysem, (h, d), y_dev(d)
+        )
+
+    def to_z(k, h, d):
+        src, dst = ((yb, zrecv), (pzsend, pzrecv))[k]
+        return remote(
+            src.at[h, :, at(z_at(d), 128)], dst.at[h, d], rzsem, (k, h, d), z_dev(d)
+        )
+
+    def gather_z_copy(k, h, d, block):
+        ref = (ub, ob)[k]
+        return remote(
+            ref.at[h, rows, at(z, 128)], ref.at[h, rows, at(block, 128)], azsem, (k, h, d), z_dev(d)
+        )
+
+    def gather_x_copy(k, h, d, block):
+        ref = (ub, ob)[k]
         r = pl.ds(pl.multiple_of(c * 64 + block * 16, 16), 16)
-        return remote(ref.at[rows, :], ref.at[r, :], axsem, (k, d), x_dev(d))
-
-    def gather_core_copy(k, d, half):
-        ref = (ub, out)[k]
+        return remote(ref.at[h, rows, :], ref.at[h, r, :], axsem, (k, h, d), x_dev(d))
+
+    def gather_core_copy(k, h, d, half):
+        ref = (ub, ob)[k]
         block = lax.rem(x + 4 - d, 4)
         src = pl.ds(pl.multiple_of(c * 64 + block * 16, 16), 16)
         dst = pl.ds(pl.multiple_of(half * 64 + block * 16, 16), 16)
-        return remote(ref.at[src, :], ref.at[dst, :], acsem, (k, d), core_dev)
+        return remote(ref.at[h, src, :], ref.at[h, dst, :], acsem, (k, h, d), core_dev)
+
+    def out_copy(h, block):
+        return pltpu.make_async_copy(
+            ob.at[h, :, pl.ds(block * 512, 512)],
+            out.at[:, pl.ds(block * 1024 + h * 512, 512)],
+            osem.at[h, block],
+        )
 
     def farthest_first(k):
         j = lax.div(k + 1, 2)
         return 8 + j * (1 - 2 * lax.rem(k, 2))
 
-    def gather(k, under_z=None, under_x=None):
+    def send_z(k, h):
         @pl.loop(0, 15)
         def _(i):
-            d = farthest_first(i)
-            gather_z_copy(k, d, z).start()
-
-        if under_z is not None:
-            under_z()
-
+            to_z(k, h, farthest_first(i)).start()
+
+    def take_z(k, h):
         @pl.loop(1, 16)
         def _(d):
-            gather_z_copy(k, d, z_at(16 - d)).wait_recv()
-
-        for d in (2, 1, 3):
-            gather_x_copy(k, d, x).start()
-        gather_core_copy(k, 0, c).start()
+            to_z(k, h, d).wait_recv()
+
+    def gather_begin(k, h):
+        @pl.loop(0, 15)
+        def _(i):
+            gather_z_copy(k, h, farthest_first(i), z).start()
+
+    def gather_rest(k, under_x=None):
+        for h in (0, 1):
+
+            @pl.loop(1, 16)
+            def _(d):
+                gather_z_copy(k, h, d, z_at(16 - d)).wait_recv()
+
+            for d in (2, 1, 3):
+                gather_x_copy(k, h, d, x).start()
+            gather_core_copy(k, h, 0, c).start()
         if under_x is not None:
             under_x()
-        for d in (1, 3, 2):
-            gather_x_copy(k, d, x_at(4 - d)).wait_recv()
-            gather_core_copy(k, d, c).start()
+        for h in (0, 1):
+            for d in (1, 3, 2):
+                gather_x_copy(k, h, d, x_at(4 - d)).wait_recv()
+                gather_core_copy(k, h, d, c).start()
+
+    def gather_end(k, h):
         for d in (0, 1, 3, 2):
-            gather_core_copy(k, d, 1 - c).wait_recv()
+            gather_core_copy(k, h, d, 1 - c).wait_recv()
 
     def tell(i):
         pl.semaphore_signal(left.at[i], inc=1, device_id=z_dev(2**i), device_id_type=MESH)
@@ -222,70 +268,56 @@
     tell(1)
     for d in (1, 3, 2):
         grad_copy(d, 1 - c, y_at(4 - d)).wait_recv()
-    half = lax.dot_general(
-        gall[1 - c].reshape(256, 512), kvv[...], NT, preferred_element_type=F32
-    )
-    usend[...] = half.astype(BF16).reshape(4, 64, 1024)
-    ucore = remote(usend, crecv, rcsem, (0,), core_dev)
-    ucore.start()
+
+    def upstream_part(half, h):
+        return lax.dot_general(
+            gall[half].reshape(256, 512), kvv[pl.ds(h * 512, 512), :], NT, preferred_element_type=F32
+        ).reshape(4, 64, 512)
+
+    for h in (0, 1):
+        usend[h] = upstream_part(1 - c, h).astype(BF16)
+        to_core(0, h).start()
     heard(1)
     tell(2)
     for d in (1, 3, 2):
         grad_copy(d, c, y_at(4 - d)).wait_recv()
-    for k, way, p in ((0, 0, 0), (0, 1, 1), (0, 0, 1), (0, 1, 0), (1, 0, 0), (1, 1, 1)):
-        near_copy(k, way, p, y).start()
-    uown[...] = lax.dot_general(
-        gall[c].reshape(256, 512), kvv[...], NT, preferred_element_type=F32
-    ).reshape(4, 64, 1024)
-    ucore.wait_recv()
-    for r in range(4):
-        xsend[r] = (uown[r] + crecv[r].astype(F32)).astype(BF16)
-
-    def ux_copy(d):
-        return remote(xsend.at[:, at(x_at(d), 16), :], xrecv.at[d], rxsem, (0, d), x_dev(d))
-
-    for d in (2, 1, 3):
-        ux_copy(d).start()
+    for way, p in ((0, 0), (1, 1), (0, 1), (1, 0)):
+        near_copy(0, way, p, y).start()
+    for h in (0, 1):
+        uown[h] = upstream_part(c, h)
+        to_core(0, h).wait_recv()
+        for r in range(4):
+            xsend[h, r] = (uown[h, r] + crecv[h, r].astype(F32)).astype(BF16)
+        for d in (2, 1, 3):
+            to_x(0, h, d).start()
     heard(2)
 
     @pl.loop(1, 8)
     def _(d):
         lo_copy(0, d, t).start()
 
-    @pl.loop(1, 8)
-    def _(d):
-        lo_copy(1, d, t).start()
-
-
-    for d in (1, 3, 2):
-        ux_copy(d).wait_recv()
-    for r in range(4):
-        total = uown[r, xrows, :] + crecv[r, xrows, :].astype(F32)
-        for d in range(1, 4):
-            total = total + xrecv[d, r].astype(F32)
-        ysend[r] = total.astype(BF16)
-
-    def uy_copy(d, block):
-        return remote(ysend.at[y_at(d)], yb.at[:, at(block, 1024)], rysem, (d,), y_dev(d))
-
-    for d in (2, 1, 3):
-        uy_copy(d, y).start()
-    yb[:, at(y, 1024)] = ysend[y]
-    relay(0)
-    relay(1)
-    for k, way, p in ((1, 0, 1), (1, 1, 0), (2, 0, 0), (2, 1, 1), (2, 0, 1), (2, 1, 0)):
-        near_copy(k, way, p, y).start()
-
-    for d in (1, 3, 2):
-        uy_copy(d, y_at(4 - d)).wait_recv()
-
-    def uz_copy(d):
-        return remote(yb.at[:, at(z_at(d), 256)], zrecv.at[d], rzsem, (0, d), z_dev(d))
-
-    @pl.loop(0, 15)
-    def _(i):
-        uz_copy(farthest_first(i)).start()
-
+    for h in (0, 1):
+        for d in (1, 3, 2):
+            to_x(0, h, d).wait_recv()
+        for r in range(4):
+            total = uown[h, r, xrows, :] + crecv[h, r, xrows, :].astype(F32)
+            for d in range(1, 4):
+                total = total + xrecv[h, d, r].astype(F32)
+            ysend[h, r] = total.astype(BF16)
+        for d in (2, 1, 3):
+            to_y(h, d, y).start()
+        yb[h, :, at(y, 512)] = ysend[h, y]
+        if h == 0:
+            relay(0)
+    for h in (0, 1):
+        for d in (1, 3, 2):
+            to_y(h, d, y_at(4 - d)).wait_recv()
+        send_z(0, h)
+        if h == 0:
+            for way, p in ((0, 0), (1, 1), (0, 1), (1, 0)):
+                near_copy(1, way, p, y).start()
+    for way, p in ((0, 0), (1, 1), (0, 1), (1, 0)):
+        near_copy(2, way, p, y).start()
     own[2].wait()
 
     @pl.loop(1, 8)
@@ -294,25 +326,15 @@
 
     for d in (2, 1, 3):
         side_x_copy(0, d, x).start()
-    own[3].wait()
-
-    @pl.loop(1, 8)
-    def _(d):
-        lo_copy(1, d, lax.rem(t + 8 - d, 8)).wait_recv()
-
-    for d in (2, 1, 3):
-        enc_y_copy(d, y).start()
-    ee[y, rows, :] = eb[:, at(y, 1024)]
-
-    @pl.loop(1, 16)
-    def _(d):
-        uz_copy(d).wait_recv()
-
-    total = yb[:, at(z, 256)].astype(F32)
-    for d in range(1, 16):
-        total = total + zrecv[d].astype(F32)
-    upf[...] = total
-    ub[rows, at(z, 256)] = total.astype(BF16)
+    relay(1)
+    for h in (0, 1):
+        take_z(0, h)
+        total = yb[h, :, at(z, 128)].astype(F32)
+        for d in range(1, 16):
+            total = total + zrecv[h, d].astype(F32)
+        upf[h] = total
+        ub[h, rows, at(z, 128)] = total.astype(BF16)
+        gather_begin(0, h)
 
     def normalize():
         relay(2)
@@ -335,6 +357,10 @@
             nb[:, columns] = (values * gf[j : j + 1, :]).astype(BF16)
 
     def hidden_units():
+        @pl.loop(1, 8)
+        def _(d):
+            lo_copy(1, d, t).start()
+
         weight_here(0)
         weight_here(1)
         pre[...] = jnp.dot(nb[...], gu[...], preferred_element_type=F32)
@@ -356,23 +382,38 @@
             for k in range(2):
                 kvg[at(i, 256), k, :] = total[:, k * 256 : k * 256 + 256]
 
-    gather(0, normalize, hidden_units)
-
+    normalize()
+    gather_rest(0, hidden_units)
     weight_here(2)
-    hidden = lax.dot_general(ub[...], db[...], NT, preferred_element_type=F32)
+    own[7].wait()
+
+    gather_end(0, 0)
+    hidden = lax.dot_general(ub[0], db[0], NT, preferred_element_type=F32)
+    gather_end(0, 1)
+    hidden = hidden + lax.dot_general(ub[1], db[1], NT, preferred_element_type=F32)
     grads = (jnp.concatenate([hidden, hidden], axis=1) * act[...]).astype(BF16)
     gg[...] = grads
-    def term(half, block):
+    def term(half, h, block):
         return lax.dot_general(
-            gg[at(half, 64), :], gu[pl.ds(block * 1024, 1024), :], NT, preferred_element_type=F32
+            gg[at(half, 64), :],
+            gu[pl.ds(block * 1024 + h * 512, 512), :],
+            NT,
+            preferred_element_type=F32,
         )
 
-    for block in range(4):
-        psend[:, pl.ds(block * 1024, 1024)] = term(1 - c, block).astype(BF16)
-    pcore = remote(psend, pcrecv, rcsem, (1,), core_dev)
-    pcore.start()
-    for block in range(4):
-        pown[:, pl.ds(block * 1024, 1024)] = term(c, block)
+    for h in (0, 1):
+        for block in range(4):
+            psend[h, :, pl.ds(block * 512, 512)] = term(1 - c, h, block).astype(BF16)
+        to_core(1, h).start()
+    for h in (0, 1):
+        for block in range(4):
+            pown[h, :, pl.ds(block * 512, 512)] = term(c, h, block)
+        to_core(1, h).wait_recv()
+        for i in range(4):
+            r = pl.ds(i * 16, 16)
+            pxsend[h, r, :] = (pown[h, r, :] + pcrecv[h, r, :].astype(F32)).astype(BF16)
+        for d in (2, 1, 3):
+            to_x(1, h, d).start()
 
     product = gg[...].astype(F32) * pre[...]
     high = product.astype(BF16)
@@ -394,16 +435,27 @@
     def _(i):
         sz_copy(farthest_first(i)).start()
 
-    pcore.wait_recv()
-    for i in range(4):
-        r = pl.ds(i * 16, 16)
-        pxsend[r, :] = (pown[r, :] + pcrecv[r, :].astype(F32)).astype(BF16)
-
-    def px_copy(d):
-        return remote(pxsend.at[at(x_at(d), 16), :], pxrecv.at[d], rxsem, (1, d), x_dev(d))
+    own[3].wait()
+
+    @pl.loop(1, 8)
+    def _(d):
+        lo_copy(1, d, lax.rem(t + 8 - d, 8)).wait_recv()
 
     for d in (2, 1, 3):
-        px_copy(d).start()
+        enc_y_copy(d, y).start()
+    ee[y, rows, :] = eb[:, at(y, 1024)]
+
+    for h in (0, 1):
+        for d in (1, 3, 2):
+            to_x(1, h, d).wait_recv()
+        for i in range(2):
+            columns = pl.ds(i * 1024, 1024)
+            total = pown[h, xrows, columns] + pcrecv[h, xrows, columns].astype(F32)
+            for d in range(1, 4):
+                total = total + pxrecv[h, d, :, columns].astype(F32)
+            pzsend[h, :, columns] = total.astype(BF16)
+        send_z(1, h)
+
     @pl.loop(1, 16)
     def _(d):
         sz_copy(d).wait_recv()
@@ -414,22 +466,6 @@
     sxsend[...] = total
     for d in (2, 1, 3):
         sx_copy(d).start()
-    for d in (1, 3, 2):
-        px_copy(d).wait_recv()
-    for i in range(4):
-        columns = pl.ds(i * 1024, 1024)
-        total = pown[xrows, columns] + pcrecv[xrows, columns].astype(F32)
-        for d in range(1, 4):
-            total = total + pxrecv[d, :, columns].astype(F32)
-        pzsend[:, columns] = total.astype(BF16)
-
-    def pz_copy(d):
-        return remote(pzsend.at[:, at(z_at(d), 256)], pzrecv.at[d], rzsem, (1, d), z_dev(d))
-
-    @pl.loop(0, 15)
-    def _(i):
-        pz_copy(farthest_first(i)).start()
-
     for d in (1, 3, 2):
         enc_y_copy(d, y_at(4 - d)).wait_recv()
     for d in (2, 1, 3):
@@ -444,22 +480,27 @@
     mine = lax.broadcasted_iota(jnp.int32, (16, 128), 1) == token
     stat = jnp.sum(jnp.where(mine, jnp.broadcast_to(stat_row, (16, 128)), 0.0), axis=1, keepdims=True)
     scale = rsb[rows, 0:1]
-    values = xb[rows, at(z, 256)].astype(F32)
-    gain_here = jnp.concatenate([gf[pl.ds(2 * z, 1), :], gf[pl.ds(2 * z + 1, 1), :]], axis=1)
-    base = upf[...] - values * (scale * scale) * (stat * (1.0 / 4096.0))
-
-    @pl.loop(1, 16)
-    def _(d):
-        pz_copy(d).wait_recv()
-
+    bases, gains = [], []
+    for h in (0, 1):
+        column = lax.div(z, 4) * 8 + h * 4 + lax.rem(z, 4)
+        values = xb[rows, at(column, 128)].astype(F32)
+        bases.append(upf[h] - values * (scale * scale) * (stat * (1.0 / 4096.0)))
+        gains.append(scale * gf[pl.ds(column, 1), :])
+    for h in (0, 1):
+        take_z(1, h)
+        total = pzsend[h, :, at(z, 128)].astype(F32)
+        for d in range(1, 16):
+            total = total + pzrecv[h, d].astype(F32)
+        ob[h, rows, at(z, 128)] = (bases[h] + gains[h] * total).astype(BF16)
+        gather_begin(1, h)
     for d in (1, 3, 2):
         side_x_copy(1, d, x_at(4 - d)).wait_recv()
     side_core_copy(1, c).start()
-    total = pzsend[:, at(z, 256)].astype(F32)
-    for d in range(1, 16):
-        total = total + pzrecv[d].astype(F32)
-    out[rows, at(z, 256)] = (base + scale * gain_here * total).astype(BF16)
-    gather(1, kv_rows)
+    gather_rest(1, kv_rows)
+    for h in (0, 1):
+        gather_end(1, h)
+        for block in range(4):
+            out_copy(h, block).start()
 
     for d in range(1, 4):
         for h in (0, 1):
@@ -467,23 +508,24 @@
         enc_y_copy(d, y).wait_send()
         for k in (0, 1):
             side_x_copy(k, d, x).wait_send()
-            gather_x_copy(k, d, x).wait_send()
-        ux_copy(d).wait_send()
-        uy_copy(d, y).wait_send()
-        px_copy(d).wait_send()
+            for h in (0, 1):
+                gather_x_copy(k, h, d, x).wait_send()
+                to_x(k, h, d).wait_send()
+        to_y(0, d, y).wait_send()
+        to_y(1, d, y).wait_send()
         sx_copy(d).wait_send()
     for k in (0, 1):
         side_core_copy(k, c).wait_send()
-        for d in range(4):
-            gather_core_copy(k, d, c).wait_send()
+        for h in (0, 1):
+            to_core(k, h).wait_send()
+            for d in range(4):
+                gather_core_copy(k, h, d, c).wait_send()
     for k in range(3):
         for p in (0, 1):
             near_copy(k, 0, p, y).wait_send()
             near_copy(k, 1, p, y).wait_send()
             far_copy(k, p).wait_send()
-    ucore.wait_send()
     score.wait_send()
-    pcore.wait_send()
 
     @pl.loop(1, 8)
     def _(d):
@@ -492,11 +534,15 @@
 
     @pl.loop(1, 16)
     def _(d):
-        uz_copy(d).wait_send()
-        pz_copy(d).wait_send()
         sz_copy(d).wait_send()
-        gather_z_copy(0, d, z).wait_send()
-        gather_z_copy(1, d, z).wait_send()
+        for k in (0, 1):
+            for h in (0, 1):
+                to_z(k, h, d).wait_send()
+                gather_z_copy(k, h, d, z).wait_send()
+
+    for h in (0, 1):
+        for block in range(4):
+            out_copy(h, block).wait()
 
 
 def on_device(
@@ -512,24 +558,25 @@
             jax.ShapeDtypeStruct((1024, 2, 256), BF16),
         ),
         in_specs=[anywhere] * 7 + [vmem],
-        out_specs=(vmem, vmem),
+        out_specs=(anywhere, vmem),
         scratch_shapes=[
             pltpu.VMEM((128, 2, 256), BF16),
             pltpu.VMEM((1024, 2, 256), BF16),
             pltpu.VMEM((2, 4, 64, 512), BF16),
             pltpu.VMEM((1024, 512), BF16),
-            pltpu.VMEM((4, 64, 1024), BF16),
-            pltpu.VMEM((4, 64, 1024), F32),
-            pltpu.VMEM((4, 64, 1024), BF16),
-            pltpu.VMEM((4, 64, 1024), BF16),
-            pltpu.VMEM((4, 4, 16, 1024), BF16),
-            pltpu.VMEM((4, 16, 1024), BF16),
-            pltpu.VMEM((16, 4096), BF16),
-            pltpu.VMEM((16, 16, 256), BF16),
-            pltpu.VMEM((16, 256), F32),
-            pltpu.VMEM((128, 4096), BF16),
+            pltpu.VMEM((2, 4, 64, 512), BF16),
+            pltpu.VMEM((2, 4, 64, 512), F32),
+            pltpu.VMEM((2, 4, 64, 512), BF16),
+            pltpu.VMEM((2, 4, 64, 512), BF16),
+            pltpu.VMEM((2, 4, 4, 16, 512), BF16),
+            pltpu.VMEM((2, 4, 16, 512), BF16),
+            pltpu.VMEM((2, 16, 2048), BF16),
+            pltpu.VMEM((2, 16, 16, 128), BF16),
+            pltpu.VMEM((2, 16, 128), F32),
+            pltpu.VMEM((2, 128, 2048), BF16),
             pltpu.VMEM((4096, 256), BF16),
-            pltpu.VMEM((128, 4096), BF16),
+            pltpu.VMEM((2, 128, 2048), BF16),
+            pltpu.VMEM((2, 128, 2048), BF16),
             pltpu.VMEM((128, 4096), BF16),
             pltpu.VMEM((128, 4096), BF16),
             pltpu.VMEM((128, 128), F32),
@@ -539,13 +586,13 @@
             pltpu.VMEM((128, 256), F32),
             pltpu.VMEM((128, 256), F32),
             pltpu.VMEM((128, 256), BF16),
-            pltpu.VMEM((64, 4096), BF16),
-            pltpu.VMEM((64, 4096), F32),
-            pltpu.VMEM((64, 4096), BF16),
-            pltpu.VMEM((64, 4096), BF16),
-            pltpu.VMEM((4, 16, 4096), BF16),
-            pltpu.VMEM((16, 4096), BF16),
-            pltpu.VMEM((16, 16, 256), BF16),
+            pltpu.VMEM((2, 64, 2048), BF16),
+            pltpu.VMEM((2, 64, 2048), F32),
+            pltpu.VMEM((2, 64, 2048), BF16),
+            pltpu.VMEM((2, 64, 2048), BF16),
+            pltpu.VMEM((2, 4, 16, 2048), BF16),
+            pltpu.VMEM((2, 16, 2048), BF16),
+            pltpu.VMEM((2, 16, 16, 128), BF16),
             pltpu.VMEM((16, 8, 128), F32),
             pltpu.VMEM((8, 128), F32),
             pltpu.VMEM((4, 8, 128), F32),
@@ -560,16 +607,17 @@
             dma((2, 4)),
             dma((2, 2, 4)),
             dma((2, 2)),
-            dma((2, 2)),
+            dma((2, 2, 2)),
+            dma((2, 2, 2, 4)),
             dma((2, 2, 4)),
-            dma((2, 4)),
-            dma((2, 2, 16)),
-            dma((2, 2, 16)),
-            dma((2, 2, 4)),
-            dma((2, 2, 4)),
+            dma((2, 2, 2, 16)),
+            dma((2, 2, 2, 16)),
+            dma((2, 2, 2, 4)),
+            dma((2, 2, 2, 4)),
             dma((2, 16)),
             dma((2, 4)),
             dma((2,)),
+            dma((2, 4)),
         ],
         compiler_params=pltpu.CompilerParams(collective_id=0, has_side_effects=True),
     )(

time: 104 us -> 99 us (0.952)
  Pallas kernels: 100 us -> 94.8 us
    pallas_call x1, Pallas kernels: 100 us -> 94.8 us  [on_device(): pl.pallas_call(kernel, out_shape=(jax.ShapeDtypeStruct((128, 4096), BF16)...]
where the time goes in v3:
time: 99 us; the launch traced here: 98.8 us
  Pallas kernels  94.8 us (96%)
  local copies, waits for them, and re-layouts  3.35 us (3%)
    pallas_call x1, Pallas kernels, on_device(): pl.pallas_call(kernel, out_shape=(jax.ShapeDtypeStruct((128, 4096), BF16)...  94.8 us
    unnamed x4, local copies, waits for them, and re-layouts  3.35 us

profile of v3, /device:TPU:1, one launch (start us, length us, event | category | flops | bytes accessed | tf_op | source)
XLA Modules:
  0.0 98.8 jit_solution(1526064031277800666)
XLA Ops:
  0.6 94.8 %shard_map.95 = (bf16[128,4096]{1,0:T(8,128)(2,1)}, bf16[1024,2,256]{2,1,0:T(2,128)(2,1)}) custom-call(bf16[128,512]{1,0:T(8,128)(2,1)} %enc.1, bf16[128,512]{1,0:T(8,128)(2,1)} %mlp.1, bf16[128,2,256]{2,1,0:T(2,128)(2,1)} %bitcast.8, bf16[1024,2,256]{2,1,0:T(2,128)(2,1)} %bitcast.6, bf16[1024,128]{1,0:T(8,128)(2,1)} %gate.1, bf16[1024,128]{1,0:T(8,128)(2,1)} %up.1, ...), custom_call_target="tpu_custom_call" | custom-call | tf_op jit(solution)/shard_map/pallas_call | solution.py:554
  95.5 0.0 copy-start
  95.5 2.4 %copy.13 = bf16[128,4096]{1,0:T(8,128)(2,1)} copy(bf16[128,4096]{1,0:T(8,128)(2,1)} %get-tuple-element.10) | data formatting | bytes 2097152
  97.9 0.0 copy-done
  97.9 1.0 copy.14
Async XLA Ops:
  95.5 2.4 %copy-start = (bf16[1024,2,256]{2,1,0:T(2,128)(2,1)S(1)}, bf16[1024,2,256]{2,1,0:T(2,128)(2,1)}, u32[]{:S(2)}) copy-start(bf16[1024,2,256]{2,1,0:T(2,128)(2,1)} %get-tuple-element.5) | copy-start | bytes 3145732

commit v4 on v3

--- a/solution.py
+++ b/solution.py
@@ -30,9 +30,9 @@
 def kernel(
     enc, mlp, grad, kvw, gate, up, down, gain, out, kvg,
     gin, kin, gall, kvv, usend, uown, crecv, xsend, xrecv, ysend, yb, zrecv, upf, ub,
-    gu, db, ob, xb, nb, rsb, gf, eb, ee, act, pre, gg, psend, pown, pcrecv, pxsend, pxrecv, pzsend, pzrecv,
+    gu, db, ob, xb, nb, rsb, gb, gf, kvo, eb, ee, act, pre, gg, psend, pown, pcrecv, pxsend, pxrecv, pzsend, pzrecv,
     szrecv, sxsend, sxrecv, scsend, screcv, left, right,
-    lsem, gsem, wsem, msem, esem, mxsem, mcsem, rcsem, rxsem, rysem, rzsem, azsem, axsem, acsem, szsem, sxsem, scsem, osem,
+    lsem, gsem, wsem, msem, esem, mxsem, mcsem, rcsem, rxsem, rysem, rzsem, azsem, axsem, acsem, szsem, sxsem, scsem, osem, ksem,
 ):
     y, pipe, t = lax.axis_index("dp"), lax.axis_index("pipe"), lax.axis_index("tensor")
     zh, x, c = lax.div(pipe, 8), lax.rem(lax.div(pipe, 2), 4), lax.rem(pipe, 2)
@@ -92,6 +92,7 @@
         pltpu.make_async_copy(up, gu.at[at(y, 1024), pl.ds(128, 128)], lsem.at[5]),
         pltpu.make_async_copy(down.at[:, pl.ds(0, 512)], db.at[0, :, at(y, 512)], lsem.at[6]),
         pltpu.make_async_copy(down.at[:, pl.ds(512, 512)], db.at[1, :, at(y, 512)], lsem.at[7]),
+        pltpu.make_async_copy(gain, gb, lsem.at[8]),
     ]
     for copy in own:
         copy.start()
@@ -193,6 +194,9 @@
         src = pl.ds(pl.multiple_of(c * 64 + block * 16, 16), 16)
         dst = pl.ds(pl.multiple_of(half * 64 + block * 16, 16), 16)
         return remote(ref.at[h, src, :], ref.at[h, dst, :], acsem, (k, h, d), core_dev)
+
+    def kv_copy(i):
+        return pltpu.make_async_copy(kvo.at[at(i, 256)], kvg.at[at(i, 256)], ksem.at[i])
 
     def out_copy(h, block):
         return pltpu.make_async_copy(
@@ -307,8 +311,7 @@
         for d in (2, 1, 3):
             to_y(h, d, y).start()
         yb[h, :, at(y, 512)] = ysend[h, y]
-        if h == 0:
-            relay(0)
+    relay(0)
     for h in (0, 1):
         for d in (1, 3, 2):
             to_y(h, d, y_at(4 - d)).wait_recv()
@@ -336,13 +339,14 @@
         ub[h, rows, at(z, 128)] = total.astype(BF16)
         gather_begin(0, h)
 
-    def normalize():
-        relay(2)
-        for d in (1, 3, 2):
-            side_x_copy(0, d, x_at(4 - d)).wait_recv()
-        side_core_copy(0, c).start()
+    def hidden_units():
+        @pl.loop(1, 8)
+        def _(d):
+            lo_copy(1, d, t).start()
+
         side_core_copy(0, 1 - c).wait_recv()
-        gf[...] = gain[...].astype(F32)
+        own[8].wait()
+        gf[...] = gb[...].astype(F32)
 
         @pl.loop(0, 8)
         def _(i):
@@ -355,12 +359,6 @@
             columns = pl.ds(j * 128, 128)
             values = xb[:, columns].astype(F32) * rsb[...]
             nb[:, columns] = (values * gf[j : j + 1, :]).astype(BF16)
-
-    def hidden_units():
-        @pl.loop(1, 8)
-        def _(d):
-            lo_copy(1, d, t).start()
-
         weight_here(0)
         weight_here(1)
         pre[...] = jnp.dot(nb[...], gu[...], preferred_element_type=F32)
@@ -380,9 +378,13 @@
                 total = total + term.astype(BF16).astype(F32)
             total = total.astype(BF16)
             for k in range(2):
-                kvg[at(i, 256), k, :] = total[:, k * 256 : k * 256 + 256]
-
-    normalize()
+                kvo[at(i, 256), k, :] = total[:, k * 256 : k * 256 + 256]
+            kv_copy(i).start()
+
+    relay(2)
+    for d in (1, 3, 2):
+        side_x_copy(0, d, x_at(4 - d)).wait_recv()
+    side_core_copy(0, c).start()
     gather_rest(0, hidden_units)
     weight_here(2)
     own[7].wait()
@@ -467,13 +469,13 @@
     for d in (2, 1, 3):
         sx_copy(d).start()
     for d in (1, 3, 2):
+        sx_copy(d).wait_recv()
+    scsend[...] = sxsend[...] + sxrecv[1] + sxrecv[2] + sxrecv[3]
+    score.start()
+    for d in (1, 3, 2):
         enc_y_copy(d, y_at(4 - d)).wait_recv()
     for d in (2, 1, 3):
         side_x_copy(1, d, x).start()
-    for d in (1, 3, 2):
-        sx_copy(d).wait_recv()
-    scsend[...] = sxsend[...] + sxrecv[1] + sxrecv[2] + sxrecv[3]
-    score.start()
     score.wait_recv()
     stat_row = scsend[0:1, :] + screcv[0:1, :]
     token = c * 64 + x * 16 + lax.broadcasted_iota(jnp.int32, (16, 128), 0)
@@ -543,12 +545,13 @@
     for h in (0, 1):
         for block in range(4):
             out_copy(h, block).wait()
+    for i in range(4):
+        kv_copy(i).wait()
 
 
 def on_device(
     enc_out, mlp_input, grad_kv, kv_weight, gate_weight, up_weight, down_weight, norm_gain
 ):
-    vmem = pl.BlockSpec(memory_space=pltpu.VMEM)
     anywhere = pl.BlockSpec(memory_space=pl.ANY)
     dma = pltpu.SemaphoreType.DMA
     input_grad, kv_grad = pl.pallas_call(
@@ -557,8 +560,8 @@
             jax.ShapeDtypeStruct((128, 4096), BF16),
             jax.ShapeDtypeStruct((1024, 2, 256), BF16),
         ),
-        in_specs=[anywhere] * 7 + [vmem],
-        out_specs=(anywhere, vmem),
+        in_specs=[anywhere] * 8,
+        out_specs=(anywhere, anywhere),
         scratch_shapes=[
             pltpu.VMEM((128, 2, 256), BF16),
             pltpu.VMEM((1024, 2, 256), BF16),
@@ -580,7 +583,9 @@
             pltpu.VMEM((128, 4096), BF16),
             pltpu.VMEM((128, 4096), BF16),
             pltpu.VMEM((128, 128), F32),
+            pltpu.VMEM((32, 128), BF16),
             pltpu.VMEM((32, 128), F32),
+            pltpu.VMEM((1024, 2, 256), BF16),
             pltpu.VMEM((16, 4096), BF16),
             pltpu.VMEM((4, 128, 1024), BF16),
             pltpu.VMEM((128, 256), F32),
@@ -600,7 +605,7 @@
             pltpu.VMEM((8, 128), F32),
             pltpu.SemaphoreType.REGULAR((3,)),
             pltpu.SemaphoreType.REGULAR((3,)),
-            dma((8,)),
+            dma((9,)),
             dma((2, 4, 2)),
             dma((2, 3, 3, 2)),
             dma((2, 2, 8)),
@@ -618,6 +623,7 @@
             dma((2, 4)),
             dma((2,)),
             dma((2, 4)),
+            dma((4,)),
         ],
         compiler_params=pltpu.CompilerParams(collective_id=0, has_side_effects=True),
     )(

time: 99 us -> 95.6 us (0.966)
  Pallas kernels: 94.8 us -> 91.4 us
    pallas_call x1, Pallas kernels: 94.8 us -> 91.4 us  [on_device(): pl.pallas_call(kernel, out_shape=(jax.ShapeDtypeStruct((128, 4096), BF16)...]
where the time goes in v4:
time: 95.6 us; the launch traced here: 95.4 us
  Pallas kernels  91.4 us (96%)
  local copies, waits for them, and re-layouts  3.35 us (4%)
    pallas_call x1, Pallas kernels, on_device(): pl.pallas_call(kernel, out_shape=(jax.ShapeDtypeStruct((128, 4096), BF16)...  91.4 us
    unnamed x4, local copies, waits for them, and re-layouts  3.35 us

profile of v4, /device:TPU:1, one launch (start us, length us, event | category | flops | bytes accessed | tf_op | source)
XLA Modules:
  0.0 95.4 jit_solution(2424464820843989106)
XLA Ops:
  0.6 91.4 %shard_map.95 = (bf16[128,4096]{1,0:T(8,128)(2,1)}, bf16[1024,2,256]{2,1,0:T(2,128)(2,1)}) custom-call(bf16[128,512]{1,0:T(8,128)(2,1)} %enc.1, bf16[128,512]{1,0:T(8,128)(2,1)} %mlp.1, bf16[128,2,256]{2,1,0:T(2,128)(2,1)} %bitcast.8, bf16[1024,2,256]{2,1,0:T(2,128)(2,1)} %bitcast.6, bf16[1024,128]{1,0:T(8,128)(2,1)} %gate.1, bf16[1024,128]{1,0:T(8,128)(2,1)} %up.1, ...), custom_call_target="tpu_custom_call" | custom-call | tf_op jit(solution)/shard_map/pallas_call | solution.py:557
  92.1 0.0 copy-start
  92.1 2.4 %copy.13 = bf16[128,4096]{1,0:T(8,128)(2,1)} copy(bf16[128,4096]{1,0:T(8,128)(2,1)} %get-tuple-element.10) | data formatting | bytes 2097152
  94.5 0.0 copy-done
  94.5 1.0 %copy.14 = bf16[1024,2,1,256]{3,1,2,0:T(2,128)(2,1)} copy(bf16[1024,2,1,256]{3,1,2,0:T(2,128)(2,1)S(1)} %bitcast.7) | data formatting | bytes 2097152
Async XLA Ops:
  92.1 2.4 %copy-start = (bf16[1024,2,256]{2,1,0:T(2,128)(2,1)S(1)}, bf16[1024,2,256]{2,1,0:T(2,128)(2,1)}, u32[]{:S(2)}) copy-start(bf16[1024,2,256]{2,1,0:T(2,128)(2,1)} %get-tuple-element.5) | copy-start | bytes 3145732

commit v5 on v4

--- a/solution.py
+++ b/solution.py
@@ -76,13 +76,6 @@
     def greet(device):
         pl.semaphore_signal(barrier, inc=1, device_id=device, device_id_type=MESH)
 
-    for d in (1, 2, 3):
-        greet(y_dev(d))
-        greet(x_dev(d))
-    greet(core_dev)
-    greet(z_dev(1))
-    greet(z_dev(15))
-
     own = [
         pltpu.make_async_copy(grad, gin, lsem.at[0]),
         pltpu.make_async_copy(kvw, kin, lsem.at[1]),
@@ -94,8 +87,14 @@
         pltpu.make_async_copy(down.at[:, pl.ds(512, 512)], db.at[1, :, at(y, 512)], lsem.at[7]),
         pltpu.make_async_copy(gain, gb, lsem.at[8]),
     ]
-    for copy in own:
-        copy.start()
+    own[0].start()
+    for d in (1, 2, 3):
+        greet(y_dev(d))
+        greet(x_dev(d))
+    greet(core_dev)
+    greet(z_dev(1))
+    greet(z_dev(15))
+    own[1].start()
     own[0].wait()
     for h in range(2):
         for k in range(2):
@@ -260,6 +259,8 @@
     for d in (2, 1, 3):
         grad_copy(d, c, y).start()
 
+    for copy in own[2:]:
+        copy.start()
     own[1].wait()
 
     @pl.loop(0, 8)

time: 95.6 us -> 95.6 us (level)
  no operation moved by 1% of the time
where the time goes in v5:
time: 95.6 us; the launch traced here: 95.5 us
  Pallas kernels  91.5 us (96%)
  local copies, waits for them, and re-layouts  3.35 us (4%)
    pallas_call x1, Pallas kernels, on_device(): pl.pallas_call(kernel, out_shape=(jax.ShapeDtypeStruct((128, 4096), BF16)...  91.5 us
    unnamed x4, local copies, waits for them, and re-layouts  3.35 us

profile of v5, /device:TPU:1, one launch (start us, length us, event | category | flops | bytes accessed | tf_op | source)
XLA Modules:
  0.0 95.5 jit_solution(18177616264929243596)
XLA Ops:
  0.6 91.5 %shard_map.95 = (bf16[128,4096]{1,0:T(8,128)(2,1)}, bf16[1024,2,256]{2,1,0:T(2,128)(2,1)}) custom-call(bf16[128,512]{1,0:T(8,128)(2,1)} %enc.1, bf16[128,512]{1,0:T(8,128)(2,1)} %mlp.1, bf16[128,2,256]{2,1,0:T(2,128)(2,1)} %bitcast.8, bf16[1024,2,256]{2,1,0:T(2,128)(2,1)} %bitcast.6, bf16[1024,128]{1,0:T(8,128)(2,1)} %gate.1, bf16[1024,128]{1,0:T(8,128)(2,1)} %up.1, ...), custom_call_target="tpu_custom_call" | custom-call | tf_op jit(solution)/shard_map/pallas_call | solution.py:558
  92.1 0.0 copy-start
  92.1 2.4 %copy.13 = bf16[128,4096]{1,0:T(8,128)(2,1)} copy(bf16[128,4096]{1,0:T(8,128)(2,1)} %get-tuple-element.10) | data formatting | bytes 2097152
  94.5 0.0 copy-done
  94.5 1.0 %copy.14 = bf16[1024,2,1,256]{3,1,2,0:T(2,128)(2,1)} copy(bf16[1024,2,1,256]{3,1,2,0:T(2,128)(2,1)S(1)} %bitcast.7) | data formatting | bytes 2097152
Async XLA Ops:
  92.1 2.4 %copy-start = (bf16[1024,2,256]{2,1,0:T(2,128)(2,1)S(1)}, bf16[1024,2,256]{2,1,0:T(2,128)(2,1)}, u32[]{:S(2)}) copy-start(bf16[1024,2,256]{2,1,0:T(2,128)(2,1)} %get-tuple-element.5) | copy-start | bytes 3145732
